TPU v7x, 256 devices: a whole 4x4x8 slice. The times are simulated.
256 devices in a mesh: facet: 8 (over y, core), sub: 32 (over x, z).
Axes of the slice: x: 4, y: 4, z: 8, core: 2. Of those that a mesh axis runs over, the one named last changes fastest.
Arguments:
- facet_strips: bfloat16 [2, 32768, 4096], P(None, 'facet', 'sub'), may hold values from -6 to 6
- row_window: float32 [4096], replicated, may hold values from 0.25 to 1.75
- col_window: float32 [4096], P('sub'), may hold values from 0.25 to 1.75
- row_offsets: int32 [8], replicated, may hold values from 0 to 3584
- col_offsets: int32 [8], replicated, may hold values from 0 to 3584
- tile_owner: int32 [32, 8, 32, 1], P('sub', 'facet'), may hold values from 0 to 31; in each aligned block of 32 rows (0 to 31, 32 to 63, ..., all dimensions but the last counted through in order) at most 4 rows name the same one
- measured: float32 [8, 32, 128, 2, 128], P('facet', 'sub'), may hold values from -12 to 12
- vis_weight: float32 [8, 32, 128, 128], P('facet', 'sub'), may hold values from 0.1 to 1
- uvw_pixels: int32 [8, 32, 128, 3, 128], P('facet', 'sub'), may hold values from 0 to 15
- vis_count: int32 [8, 32, 128], P('facet', 'sub'), may hold values from 1 to 128
Outputs:
- facet_update: bfloat16 [2, 32768, 4096], P(None, 'facet', 'sub')
Inputs may be any that keep to these rules, and one draw needn't show every extreme that they name: Among the tiles of one row block of the subgrids of one facet index (the entries of tile_owner at one s and the 1 subgrids of one index of facet), no owner is named more than 4 times, and one owner is named exactly 4 times by some row block.
All inputs are finite; a program needn't handle non-finite values.
Results may differ from a plain program's by a relative error of at most 0.024.
Values may be sent and summed in bfloat16 or wider, within the bound.
A program may use at most 128 MiB of HBM per device.

v0:
```python
import math

import jax
import jax.numpy as jnp
import numpy as np
from jax import lax
from jax.experimental import pallas as pl
from jax.experimental.pallas import tpu as pltpu
from jax.sharding import PartitionSpec as P

SG = 512
RADIX = 64
TS = 16
LONG = 4096
SUBS = 32
FACETS = 8
CAP = 4
LANES = 128
MESH = pl.DeviceIdType.MESH
F32 = jnp.float32
BF16 = jnp.bfloat16

kernel_width = 2.5
kernel_norm = 0.565


def as_real(theta):
    cosine, sine = np.cos(theta), np.sin(theta)
    return np.block([[cosine, sine], [-sine, cosine]])


def row_tables():
    idx = np.arange(RADIX)
    first = as_real(2 * np.pi * (np.outer(idx, idx) % RADIX) / RADIX)
    second = [
        as_real(2 * np.pi * (np.outer(k1 + RADIX * idx, idx) % LONG) / LONG) / RADIX
        for k1 in range(RADIX)
    ]
    return jnp.asarray(first, BF16), jnp.asarray(np.stack(second), BF16)


def col_tables():
    high = np.outer(np.arange(16), np.arange(LANES)) % LANES
    dense = as_real(2 * np.pi * high / LANES)
    low = 2 * np.pi * np.outer(np.arange(SUBS), np.arange(LANES)) / LONG
    twist = np.stack([np.cos(low), np.sin(low)]) / 64.0
    rep = np.zeros((512, 32))
    rep[np.arange(512), np.arange(512) // 16] = 1
    sel = np.zeros((2, 16, 16, 4, 2, 16))
    for z in range(2):
        for r in range(16):
            sel[z, :, r, :, z, r] = 1
    sel = sel.reshape(512, 128)
    keep = (np.arange(512)[:, None] % 16) == (np.arange(512)[None, :] // 16 % 16)
    return (
        jnp.asarray(dense, BF16),
        jnp.asarray(twist, F32),
        jnp.asarray(rep, BF16),
        jnp.asarray(rep.T, BF16),
        jnp.asarray(sel, BF16),
        jnp.asarray(keep, BF16),
    )


def mm(first, other):
    return jnp.dot(first, other, preferred_element_type=F32)


def mm_nt(first, other):
    return lax.dot_general(first, other, (((1,), (1,)), ((), ())), preferred_element_type=F32)


def mm_tn(first, other):
    return lax.dot_general(first, other, (((0,), (0,)), ((), ())), preferred_element_type=F32)


def transform_rows(re, im, mid_re, mid_im, first, second):
    def stage_a(step, carry):
        parts = []
        for u in range(2):
            rows = pl.ds(2 * step + u, RADIX, stride=RADIX)
            parts.append(jnp.concatenate([re[rows, :], im[rows, :]], axis=0).astype(BF16))
        res = mm(first[...], jnp.concatenate(parts, axis=1))
        for u in range(2):
            rows = pl.ds(2 * step + u, RADIX, stride=RADIX)
            mid_re[rows, :] = res[:RADIX, u * LANES : (u + 1) * LANES]
            mid_im[rows, :] = res[RADIX:, u * LANES : (u + 1) * LANES]
        return carry

    lax.fori_loop(0, RADIX // 2, stage_a, 0, unroll=2)

    def stage_b(step, carry):
        rows = pl.ds(pl.multiple_of(step * RADIX, RADIX), RADIX)
        block = jnp.concatenate([mid_re[rows, :], mid_im[rows, :]], axis=0).astype(BF16)
        res = mm(second[step], block)
        out_rows = pl.ds(step, RADIX, stride=RADIX)
        re[out_rows, :] = res[:RADIX]
        im[out_rows, :] = res[RADIX:]
        return carry

    lax.fori_loop(0, RADIX, stage_b, 0, unroll=4)


def forward_kernel(offs, turn, strip, win, first, second, out, re, im, mid_re, mid_im):
    def load(step, carry):
        rows = pl.ds(pl.multiple_of(step * 128, 128), 128)
        re[rows, :] = strip[0, rows, :].astype(F32) * win[rows, :]
        im[rows, :] = strip[1, rows, :].astype(F32) * win[rows, :]
        return carry

    lax.fori_loop(0, LONG // 128, load, 0, unroll=2)
    transform_rows(re, im, mid_re, mid_im, first, second)

    def emit(step, carry):
        which, part = step // 4, step % 4
        rows = pl.ds(offs[which] + part * 128, 128)
        real, imag = re[rows, :], im[rows, :]
        cosine, sine = turn[0, which], turn[1, which]
        blocks = pl.ds(part * 8, 8)
        out[which, blocks, 0] = (cosine * real + sine * imag).astype(BF16).reshape(8, 16, LANES)
        out[which, blocks, 1] = (cosine * imag - sine * real).astype(BF16).reshape(8, 16, LANES)
        return carry

    lax.fori_loop(0, 4 * FACETS, emit, 0, unroll=2)


def backward_kernel(offs, turn, strips, win, first, second, out, re, im, mid_re, mid_im):
    def clear(step, carry):
        rows = pl.ds(pl.multiple_of(step * 128, 128), 128)
        re[rows, :] = jnp.zeros((128, LANES), F32)
        im[rows, :] = jnp.zeros((128, LANES), F32)
        return carry

    lax.fori_loop(0, LONG // 128, clear, 0, unroll=2)

    def place(step, carry):
        which, part = step // 4, step % 4
        rows = pl.ds(offs[which] + part * 128, 128)
        blocks = pl.ds(part * 8, 8)
        real = strips[which, blocks, 0].reshape(128, LANES).astype(F32)
        imag = strips[which, blocks, 1].reshape(128, LANES).astype(F32)
        cosine, sine = turn[0, which], turn[1, which]
        re[rows, :] = re[rows, :] + (cosine * real - sine * imag)
        im[rows, :] = im[rows, :] - (sine * real + cosine * imag)
        return carry

    lax.fori_loop(0, 4 * FACETS, place, 0)
    transform_rows(re, im, mid_re, mid_im, first, second)

    def emit(step, carry):
        rows = pl.ds(pl.multiple_of(step * 128, 128), 128)
        out[0, rows, :] = (re[rows, :] * win[rows, :]).astype(BF16)
        out[1, rows, :] = (-im[rows, :] * win[rows, :]).astype(BF16)
        return carry

    lax.fori_loop(0, LONG // 128, emit, 0, unroll=2)


def times(pair, cosine, sine):
    return (pair[0] * cosine - pair[1] * sine, pair[0] * sine + pair[1] * cosine)


def times_unit(pair, num, den, sign):
    num = num % den
    if num == 0:
        return pair
    if 4 * num == den:
        return (-sign * pair[1], sign * pair[0])
    if 2 * num == den:
        return (-pair[0], -pair[1])
    angle = 2 * math.pi * num / den
    return times(pair, math.cos(angle), sign * math.sin(angle))


def small_dft(items, sign):
    count = len(items)
    if count == 1:
        return items
    even = small_dft(items[0::2], sign)
    odd = small_dft(items[1::2], sign)
    odd = [times_unit(odd[i], i, count, sign) for i in range(count // 2)]
    low = [(a[0] + b[0], a[1] + b[1]) for a, b in zip(even, odd)]
    high = [(a[0] - b[0], a[1] - b[1]) for a, b in zip(even, odd)]
    return low + high


def dft_over_blocks(get, put, work, sign):
    for lo in range(8):
        items = small_dft([get(lo + 8 * hi) for hi in range(4)], sign)
        for p_lo in range(4):
            value = times_unit(items[p_lo], lo * p_lo, SUBS, sign)
            work[p_lo * 8 + lo, 0] = value[0]
            work[p_lo * 8 + lo, 1] = value[1]
    for p_lo in range(4):
        items = small_dft([(work[p_lo * 8 + lo, 0], work[p_lo * 8 + lo, 1]) for lo in range(8)], sign)
        for p_hi in range(8):
            put(p_lo + 4 * p_hi, items[p_hi])


def columns_to_tiles(blocks, phase, dense, twist, rep, sel, keep, work, folded, tiles):
    def get(s):
        pair = (blocks[s, 0].astype(F32), blocks[s, 1].astype(F32))
        return times(pair, phase[0, s : s + 1, :], -phase[1, s : s + 1, :])

    def put(p, pair):
        pair = times(pair, twist[0, p : p + 1, :], -twist[1, p : p + 1, :])
        rows = slice(p * 16, p * 16 + 16)
        folded[rows, 0:LANES] = pair[0].astype(BF16)
        folded[rows, LANES : 2 * LANES] = pair[1].astype(BF16)

    dft_over_blocks(get, put, work, -1.0)
    flat = mm_nt(dense[...], folded[...]).astype(BF16)
    stacked = jnp.concatenate(
        [
            jnp.concatenate([flat[0:16, 0:256], flat[16:32, 0:256]], axis=1),
            jnp.concatenate([flat[0:16, 256:512], flat[16:32, 256:512]], axis=1),
        ],
        axis=0,
    )
    spread = mm(rep[...], stacked).astype(BF16) * keep[...]
    tiles[...] = mm(spread, sel[...]).astype(BF16)


def tiles_to_columns(tiles, phase, dense, twist, rep_t, sel, keep, work, folded_f32, images):
    spread = mm_nt(tiles[...], sel[...]).astype(BF16) * keep[...]
    stacked = mm(rep_t[...], spread).astype(BF16)
    flat = jnp.concatenate(
        [
            jnp.concatenate([stacked[0:16, 0:256], stacked[16:32, 0:256]], axis=1),
            jnp.concatenate([stacked[0:16, 256:512], stacked[16:32, 256:512]], axis=1),
        ],
        axis=0,
    )
    folded_f32[...] = mm_tn(flat, dense[...])

    def get(p):
        rows = slice(p * 16, p * 16 + 16)
        pair = (folded_f32[rows, 0:LANES], folded_f32[rows, LANES : 2 * LANES])
        return times(pair, twist[0, p : p + 1, :], twist[1, p : p + 1, :])

    def put(s, pair):
        pair = times(pair, phase[0, s : s + 1, :], phase[1, s : s + 1, :])
        images[s, 0] = pair[0].astype(BF16)
        images[s, 1] = pair[1].astype(BF16)

    dft_over_blocks(get, put, work, 1.0)


def lane_group(shape):
    return lax.broadcasted_iota(jnp.int32, shape, 1) // 32


def unit_circle(turns):
    half = jnp.where(turns >= 128.0, turns - 256.0, turns) * (math.pi / 256.0)
    sq = half * half
    sine = 1.0 / 6227020800.0
    for term in (-1.0 / 39916800.0, 1.0 / 362880.0, -1.0 / 5040.0, 1.0 / 120.0, -1.0 / 6.0, 1.0):
        sine = sine * sq + term
    sine = sine * half
    cosine = 1.0 / 479001600.0
    for term in (-1.0 / 3628800.0, 1.0 / 40320.0, -1.0 / 720.0, 1.0 / 24.0, -0.5, 1.0):
        cosine = cosine * sq + term
    return 1.0 - 2.0 * sine * sine, 2.0 * sine * cosine


def over_pixels(values):
    return jnp.broadcast_to(values[:, None, :], (8, TS, LANES)).reshape(8 * TS, LANES)


def kernel_values(aux, weights, cols):
    pixel = (lax.broadcasted_iota(jnp.int32, (8 * TS, LANES), 0) % TS).astype(F32)
    square = (pixel - 8.0) * (pixel - 8.0)

    def one(step, carry):
        rows = pl.ds(pl.multiple_of(step * 8, 8), 8)
        turns = over_pixels(aux[5, rows, :]) * square
        turns = turns - 256.0 * jnp.floor(turns * (1.0 / 256.0))
        cosine, sine = unit_circle(turns)
        row_off = (pixel - over_pixels(aux[3, rows, :])) / kernel_width
        col_off = (pixel - over_pixels(aux[4, rows, :])) / kernel_width
        row_fall = kernel_norm * jnp.exp(-(row_off * row_off))
        col_fall = kernel_norm * jnp.exp(-(col_off * col_off))
        row_re, row_im = (row_fall * cosine).astype(BF16), (-row_fall * sine).astype(BF16)
        col_re, col_im = (col_fall * cosine).astype(BF16), (-col_fall * sine).astype(BF16)
        for half in range(2):
            which = 2 * step + half
            for slot in range(4):
                src = slice(half * 64 + slot * 16, half * 64 + slot * 16 + 16)
                lo = slice(slot * 32, slot * 32 + 16)
                hi = slice(slot * 32 + 16, slot * 32 + 32)
                weights[which, lo, 0:LANES] = row_re[src]
                weights[which, lo, LANES : 2 * LANES] = row_im[src]
                weights[which, hi, 0:LANES] = -row_im[src]
                weights[which, hi, LANES : 2 * LANES] = row_re[src]
        cols[step, :, 0:LANES] = col_re
        cols[step, :, LANES : 2 * LANES] = col_im
        return carry

    lax.fori_loop(0, SUBS // 2, one, 0)


def visit(tiles, aux, weights, cols, answers):
    group = lane_group((64, LANES))
    own = group == lax.broadcasted_iota(jnp.int32, (64, LANES), 0) // TS
    own_bf = own.astype(F32).astype(BF16)
    own_f32 = own.astype(F32)

    def one(step, carry):
        rows = pl.ds(pl.multiple_of(step * 8, 8), 8)
        parts = []
        for half in range(2):
            tile = tiles[2 * step + half]
            lhs = jnp.concatenate([tile, tile, tile, tile], axis=0) * own_bf
            parts.append(mm(lhs, weights[2 * step + half]))
        part = jnp.concatenate(parts, axis=0)
        part_re, part_im = part[:, 0:LANES], part[:, LANES : 2 * LANES]
        col_re = cols[step, :, 0:LANES].astype(F32)
        col_im = cols[step, :, LANES : 2 * LANES].astype(F32)
        pred_re = jnp.sum((col_re * part_re - col_im * part_im).reshape(8, TS, LANES), axis=1)
        pred_im = jnp.sum((col_re * part_im + col_im * part_re).reshape(8, TS, LANES), axis=1)
        weight = aux[2, rows, :]
        res_re = over_pixels(weight * (aux[0, rows, :] - pred_re))
        res_im = over_pixels(weight * (aux[1, rows, :] - pred_im))
        back_re = (col_re * res_re + col_im * res_im).astype(BF16)
        back_im = (col_re * res_im - col_im * res_re).astype(BF16)
        back = jnp.concatenate([back_re, back_im], axis=1)
        for half in range(2):
            grid = mm_nt(back[half * 64 : half * 64 + 64], weights[2 * step + half]) * own_f32
            tile = (grid[0:16] + grid[16:32]) + (grid[32:48] + grid[48:64])
            answers[2 * step + half] = tile.astype(BF16)
        return carry

    lax.fori_loop(0, SUBS // 2, one, 0)


def routing(own_lane, own_col, out_rows, back_rows):
    def one(step, carry):
        start = pl.multiple_of(step * 64, 64)
        rows = pl.ds(start, 64)
        row = lax.broadcasted_iota(jnp.int32, (64, 512), 0)
        lane = lax.broadcasted_iota(jnp.int32, (64, 512), 1)
        same = row % TS == lane % TS
        to_owner = same & (own_lane[0:1, :] == row // TS + step * 4)
        owner = own_col[rows, :]
        to_tile = same & (jnp.concatenate([owner] * 4, axis=1) == lane // TS)
        out_rows[rows, :] = to_owner.astype(F32).astype(BF16)
        back_rows[rows, :] = to_tile.astype(F32).astype(BF16)
        return carry

    lax.fori_loop(0, 8, one, 0)


def add_blocks(dst, sources, lo, count):
    def one(step, carry):
        total = sources[0][lo + step].astype(F32)
        for src in sources[1:]:
            total = total + src[lo + step].astype(F32)
        dst[lo + step] = total.astype(BF16)
        return carry

    lax.fori_loop(0, count, one, 0, unroll=4)


def middle_kernel(
    mine, phase, aux, own_lane, own_col, rank, dense, twist, rep, rep_t, sel, keep,
    out,
    pair_buf, sums, carry_a, carry_b, from_dn, from_up, total, gathered,
    work, folded, folded_f32, tiles, outgoing, arrived, answers, returned, my_tiles, images,
    weights, cols, out_rows, back_rows,
    pair_s, pair_r, ring_s, ring_r, send_s, first_r, tile_r, back_r, image_r, gath_s, gath_r,
):
    me = lax.axis_index("sub")
    facet = lax.axis_index("facet")
    core, chip = lax.rem(facet, 2), facet // 2
    sib = facet + 1 - 2 * core
    up, dn = lax.rem(facet + 2, FACETS), lax.rem(facet + 6, FACETS)
    opp = lax.rem(facet + 4, FACETS)
    low, high = pl.ds(0, 16), pl.ds(16, 16)

    barrier = pltpu.get_barrier_semaphore()

    def greet(step, carry):
        pl.semaphore_signal(barrier, inc=1, device_id={"sub": lax.rem(me + step, SUBS)}, device_id_type=MESH)
        return carry

    for peer in (sib, up, dn):
        pl.semaphore_signal(barrier, inc=1, device_id={"facet": peer}, device_id_type=MESH)
    lax.fori_loop(1, SUBS, greet, 0)
    pl.semaphore_wait(barrier, SUBS + 2)

    def to_facet(src, dst, ssem, rsem, peer):
        return pltpu.make_async_remote_copy(
            src_ref=src, dst_ref=dst, send_sem=ssem, recv_sem=rsem,
            device_id={"facet": peer}, device_id_type=MESH,
        )

    pairs = {}
    for hop in (2, 1, 3, 0):
        target = 2 * lax.rem(chip + hop, 4) + 1 - core
        pairs[hop] = to_facet(mine.at[target], pair_buf.at[hop], pair_s.at[hop], pair_r.at[hop], sib)
        pairs[hop].start()

    def merge_pair(hop):
        pairs[hop].wait_recv()
        target = 2 * lax.rem(chip + hop, 4) + core
        add_blocks(sums.at[hop], [mine.at[target], pair_buf.at[hop]], 0, SUBS)

    merge_pair(2)
    ring = [
        to_facet(sums.at[2, low], carry_a, ring_s.at[0], ring_r.at[0], up),
        to_facet(sums.at[2, high], carry_b, ring_s.at[1], ring_r.at[1], dn),
        to_facet(sums.at[1, high], from_dn.at[high], ring_s.at[2], ring_r.at[2], up),
        to_facet(sums.at[3, low], from_up.at[low], ring_s.at[3], ring_r.at[3], dn),
        to_facet(sums.at[1, low], from_dn.at[low], ring_s.at[4], ring_r.at[4], up),
        to_facet(sums.at[3, high], from_up.at[high], ring_s.at[5], ring_r.at[5], dn),
    ]
    ring[0].start()
    ring[1].start()
    merge_pair(1)
    ring[2].start()
    merge_pair(3)
    ring[3].start()
    kernel_values(aux, weights, cols)
    routing(own_lane, own_col, out_rows, back_rows)
    ring[0].wait_recv()
    add_blocks(sums.at[1, low], [sums.at[1, low], carry_a], 0, 16)
    ring[4].start()
    ring[1].wait_recv()
    add_blocks(sums.at[3, high], [sums.at[3, high], carry_b], 0, 16)
    ring[5].start()
    pairs[0].wait_recv()
    for step in (2, 3, 4, 5):
        ring[step].wait_recv()
    own_target = 2 * chip + core
    add_blocks(total, [mine.at[own_target], pair_buf.at[0], from_dn, from_up], 0, SUBS)

    def swap(src_of, dst, kind, rsem):
        def copy_to(peer, slot):
            return pltpu.make_async_remote_copy(
                src_ref=src_of.at[peer], dst_ref=dst.at[slot],
                send_sem=send_s.at[kind, peer], recv_sem=rsem.at[slot],
                device_id={"sub": peer}, device_id_type=MESH,
            )

        def send(step, carry):
            copy_to(lax.rem(me + step, SUBS), me).start()
            return carry

        def receive(step, carry):
            peer = lax.rem(me + SUBS - step, SUBS)
            copy_to(peer, peer).wait_recv()
            return carry

        def drain(step, carry):
            copy_to(lax.rem(me + step, SUBS), me).wait_send()
            return carry

        lax.fori_loop(1, SUBS, send, 0)
        dst[me] = src_of[me]
        lax.fori_loop(1, SUBS, receive, 0)
        return lambda: lax.fori_loop(1, SUBS, drain, 0)

    drains = [swap(total, gathered, 0, first_r)]
    columns_to_tiles(gathered, phase, dense, twist, rep, sel, keep, work, folded, tiles)
    outgoing[...] = mm(out_rows[...], tiles[...] * rank[...]).astype(BF16).reshape(SUBS, TS, LANES)
    drains.append(swap(outgoing, arrived, 1, tile_r))
    visit(arrived, aux, weights, cols, answers)
    drains.append(swap(answers, returned, 2, back_r))
    answer = returned[...].reshape(SUBS * TS, LANES)
    my_tiles[...] = mm(back_rows[...], answer).astype(BF16) * rank[...]
    tiles_to_columns(my_tiles, phase, dense, twist, rep_t, sel, keep, work, folded_f32, images)
    drains.append(swap(images, out.at[facet], 3, image_r))

    def share(index, src, peer):
        return to_facet(src, src, gath_s.at[index], gath_r.at[index], peer)

    own = out.at[facet]
    sends = [share(0, own, up), share(1, own, dn), share(2, own, sib)]
    for copy in sends:
        copy.start()

    def arrives(index, ref):
        share(index, ref, sib).wait_recv()

    arrives(0, out.at[dn])
    onward = [share(3, out.at[dn, low], up), share(5, out.at[dn], sib)]
    for copy in onward:
        copy.start()
    arrives(1, out.at[up])
    more = [share(4, out.at[up, high], dn), share(6, out.at[up], sib)]
    for copy in more:
        copy.start()
    arrives(3, out.at[opp, low])
    last = [share(7, out.at[opp, low], sib)]
    last[0].start()
    arrives(4, out.at[opp, high])
    last.append(share(8, out.at[opp, high], sib))
    last[1].start()
    other = 1 - 2 * core
    arrives(2, out.at[sib])
    arrives(5, out.at[dn + other])
    arrives(6, out.at[up + other])
    arrives(7, out.at[opp + other, low])
    arrives(8, out.at[opp + other, high])
    for copy in sends + onward + more + last + ring:
        copy.wait_send()
    for hop in range(4):
        pairs[hop].wait_send()
    for drain in drains:
        drain()


def vmem_specs(count):
    return [pl.BlockSpec(memory_space=pltpu.VMEM)] * count


def smem_specs(count):
    return [pl.BlockSpec(memory_space=pltpu.SMEM)] * count


BIG = 60 * 1024 * 1024
STRIPS = (FACETS, SUBS, 2, 16, LANES)


def rows_call(body, out_shape):
    return pl.pallas_call(
        body,
        out_shape=out_shape,
        in_specs=smem_specs(2) + vmem_specs(4),
        out_specs=pl.BlockSpec(memory_space=pltpu.VMEM),
        scratch_shapes=[pltpu.VMEM((LONG, LANES), F32)] * 4,
        compiler_params=pltpu.CompilerParams(vmem_limit_bytes=BIG),
    )


def middle_call():
    block = (SUBS, 2, 16, LANES)
    half = (16, 2, 16, LANES)
    tile = (SUBS, 16, LANES)
    vm = pltpu.VMEM
    dma = pltpu.SemaphoreType.DMA
    return pl.pallas_call(
        middle_kernel,
        out_shape=jax.ShapeDtypeStruct(STRIPS, BF16),
        in_specs=vmem_specs(12),
        out_specs=pl.BlockSpec(memory_space=pltpu.VMEM),
        scratch_shapes=[
            vm((4,) + block, BF16), vm((4,) + block, BF16), vm(half, BF16), vm(half, BF16),
            vm(block, BF16), vm(block, BF16), vm(block, BF16), vm(block, BF16),
            vm(block, F32), vm((512, 256), BF16), vm((512, 256), F32), vm((512, LANES), BF16),
            vm(tile, BF16), vm(tile, BF16), vm(tile, BF16), vm(tile, BF16),
            vm((512, LANES), BF16), vm(block, BF16),
            vm((SUBS, LANES, 2 * LANES), BF16), vm((SUBS // 2, LANES, 2 * LANES), BF16),
            vm((512, 512), BF16), vm((512, 512), BF16),
            dma((4,)), dma((4,)), dma((6,)), dma((6,)), dma((4, SUBS)),
            dma((SUBS,)), dma((SUBS,)), dma((SUBS,)), dma((SUBS,)), dma((9,)), dma((9,)),
        ],
        compiler_params=pltpu.CompilerParams(
            vmem_limit_bytes=BIG, collective_id=0, has_side_effects=True
        ),
    )


def route_tables(owners):
    owners = owners.reshape(SUBS)
    same = owners[:, None] == owners[None, :]
    earlier = jnp.arange(SUBS)[None, :] < jnp.arange(SUBS)[:, None]
    rank = jnp.sum((same & earlier).astype(jnp.int32), axis=1)
    owners = jnp.repeat(owners.reshape(16, 2).T.reshape(SUBS), TS)
    rank = jnp.repeat(rank.reshape(16, 2).T.reshape(SUBS), TS)
    group = jnp.arange(LANES, dtype=jnp.int32) // 32
    return (
        jnp.broadcast_to(owners[None, :], (8, 512)),
        jnp.broadcast_to(owners[:, None], (512, LANES)),
        (rank[:, None] == group[None, :]).astype(BF16),
    )


def per_device(
    facet_strips, row_window, col_window, row_offsets, col_offsets,
    tile_owner, measured, vis_weight, uvw_pixels, vis_count,
):
    facet = lax.axis_index("facet")
    first, second = row_tables()
    dense, twist, rep, rep_t, sel, keep = col_tables()
    win = row_window[:, None] * col_window[None, :]
    turns = (facet * row_offsets % FACETS).astype(F32) * (2.0 * math.pi / FACETS)
    turn = jnp.stack([jnp.cos(turns), jnp.sin(turns)])
    start = lax.dynamic_index_in_dim(col_offsets, facet, keepdims=False)
    column = jnp.arange(LONG, dtype=jnp.int32).reshape(SUBS, LANES)
    angle = (column * start % LONG).astype(F32) * (2.0 * math.pi / LONG)
    phase = jnp.stack([jnp.cos(angle), jnp.sin(angle)])
    live = jnp.arange(LANES, dtype=jnp.int32)[None, :] < vis_count[0, 0][:, None]
    weight = jnp.where(live, vis_weight[0, 0], 0.0)
    pixels = uvw_pixels[0, 0].astype(F32)
    aux = jnp.stack(
        [measured[0, 0, :, 0], measured[0, 0, :, 1], weight, pixels[:, 0], pixels[:, 1], pixels[:, 2]]
    )
    own_lane, own_col, rank = route_tables(tile_owner)
    contributions = rows_call(forward_kernel, jax.ShapeDtypeStruct(STRIPS, BF16))(
        row_offsets, turn, facet_strips, win, first, second
    )
    strips = middle_call()(
        contributions, phase, aux, own_lane, own_col, rank, dense, twist, rep, rep_t, sel, keep
    )
    return rows_call(backward_kernel, jax.ShapeDtypeStruct(facet_strips.shape, BF16))(
        row_offsets, turn, strips, win, first, second
    )


def solution(mesh):
    in_specs = (
        P(None, "facet", "sub"),
        P(),
        P("sub"),
        P(),
        P(),
        P("sub", "facet", None, None),
        P("facet", "sub", None, None, None),
        P("facet", "sub", None, None),
        P("facet", "sub", None, None, None),
        P("facet", "sub", None),
    )
    return jax.shard_map(
        per_device, mesh=mesh, in_specs=in_specs, out_specs=P(None, "facet", "sub"), check_vma=False
    )
```

profile of v0, /device:TPU:1, one launch (start us, length us, event | category | flops | bytes accessed | tf_op | source)
XLA Modules:
  0.0 131.4 jit_solution(13880544509064589192)
XLA Ops:
  0.0 0.0 copy-start.2
  0.0 0.0 copy-start.1
  0.0 0.5 broadcast.168
  0.5 1.3 %reduce.3 = s32[32]{0:T(128)S(1)} reduce(s32[1,1,32,1]{2,3,1,0:T(1,128)} %param.23, s32[]{:T(128)} %broadcast.168), dimensions={0,1,3}, to_apply=%param.23.reduce_sub_computation.3 | reduce | bytes 260 | tf_op args[5]
  1.8 1.2 dynamic_slice.4
  3.1 0.9 convert_reduce_fusion
  4.0 0.7 cosine_bitcast_fusion
  4.7 0.6 pad_maximum_fusion.1.turn
  5.3 0.1 reshape.154
  5.4 0.1 copy.30
  5.5 0.1 reshape.155
  5.6 0.1 reshape_reshape.3
  5.7 0.1 copy.29
  5.8 0.1 reshape.153
  5.9 0.1 broadcast_in_dim.15
  5.9 0.1 broadcast_in_dim.30
  6.0 0.1 broadcast_in_dim.33
  6.1 0.1 eq.38
  6.2 0.6 broadcast_in_dim.31.own_lane
  6.8 0.7 fusion.8
  7.5 0.6 pad_maximum_fusion.phase
  8.1 0.8 compare_convert_fusion.rank
  8.9 1.1 fusion.14
  10.0 0.9 convert_bitcast_fusion
  11.0 0.9 broadcast_in_dim.32.own_col
  11.8 0.9 fusion.3
  12.8 0.0 copy-done.2
  12.8 0.0 copy-done.1
  12.8 0.0 copy-start
  12.9 2.0 %broadcast_multiply_fusion.win = f32[4096,128]{1,0:T(8,128)} fusion(f32[128]{0:T(128)S(1)} %copy-done.2, f32[4096]{0:T(1024)S(1)} %copy-done.1), kind=kLoop, calls=%fused_computation | loop fusion | flops 524288 | bytes 2114048 | tf_op jit(solution)/shard_map/mul | solution.py:586
  14.8 16.9 %shard_map.172.mine = bf16[8,32,2,16,128]{4,3,2,1,0:T(8,128)(2,1)} custom-call(s32[8]{0:T(128)} %offs.3, f32[2,8]{1,0:T(2,128)} %pad_maximum_fusion.1.turn, bf16[2,4096,128]{2,1,0:T(8,128)(2,1)} %strip.1, f32[4096,128]{1,0:T(8,128)} %broadcast_multiply_fusion.win, bf16[128,128]{1,0:T(8,128)(2,1)} %constant.81.clone.first, ...), custom_call_target="tpu_custom_call" | custom-call | tf_op jit(solution)/shard_map/pallas_call | solution.py:600
  31.7 0.0 copy-done
  31.7 82.1 %shard_map.173.strips = bf16[8,32,2,16,128]{4,3,2,1,0:T(8,128)(2,1)} custom-call(bf16[8,32,2,16,128]{4,3,2,1,0:T(8,128)(2,1)} %shard_map.172.mine, f32[2,32,128]{2,1,0:T(8,128)} %pad_maximum_fusion.phase, f32[6,128,128]{2,1,0:T(8,128)} %copy-done, s32[8,512]{1,0:T(8,128)} %broadcast_in_dim.31.own_lane, s32[512,128]{1,0:T(8,128)} %broadcast_in_dim.32.own_col, ...), custom_call_target="tpu_custom_call" | custom-call | tf_op jit(solution)/shard_map/pallas_call | solution.py:603
  113.8 17.6 %shard_map.174 = bf16[2,4096,128]{2,1,0:T(8,128)(2,1)} custom-call(s32[8]{0:T(128)} %offs.3, f32[2,8]{1,0:T(2,128)} %pad_maximum_fusion.1.turn, bf16[8,32,2,16,128]{4,3,2,1,0:T(8,128)(2,1)} %shard_map.173.strips, f32[4096,128]{1,0:T(8,128)} %broadcast_multiply_fusion.win, bf16[128,128]{1,0:T(8,128)(2,1)} %constant.81.clone.first, ...), custom_call_target="tpu_custom_call" | custom-call | tf_op jit(solution)/shard_map/pallas_call | solution.py:606
  (7 shorter events, 0.1 us)
Async XLA Ops:
  0.0 12.8 %copy-start.2 = (f32[128]{0:T(128)S(1)}, f32[128]{0:T(128)}, u32[]{:S(2)}) copy-start(f32[128]{0:T(128)} %param.20) | copy-start | bytes 1540
  0.0 12.8 %copy-start.1 = (f32[4096]{0:T(1024)S(1)}, f32[4096]{0:T(1024)}, u32[]{:S(2)}) copy-start(f32[4096]{0:T(1024)} %param.19) | copy-start | bytes 49156
  12.8 18.8 %copy-start = (f32[6,128,128]{2,1,0:T(8,128)}, f32[6,128,128]{2,1,0:T(8,128)S(1)}, u32[]{:S(2)}) copy-start(f32[6,128,128]{2,1,0:T(8,128)S(1)} %fusion.aux) | copy-start | bytes 1179652
where the time goes:
time: 132 us; the launch traced here: 131 us
  Pallas kernels  117 us (89%)
  other arithmetic  9.51 us (7%)
  local copies, waits for them, and re-layouts  5.21 us (4%)
    pallas_call x1, Pallas kernels, per_device(): middle_call()  82.1 us
    pallas_call x1, Pallas kernels, per_device(): rows_call(backward_kernel, jax.ShapeDtypeStruct(facet_strips.shape, BF16))  17.6 us
    pallas_call x1, Pallas kernels, per_device(): rows_call(forward_kernel, jax.ShapeDtypeStruct(STRIPS, BF16))  16.9 us

commit v1 on v0

v1 whole, which is shorter than its diff:
```python
import math

import jax
import jax.numpy as jnp
import numpy as np
from jax import lax
from jax.experimental import pallas as pl
from jax.experimental.pallas import tpu as pltpu
from jax.sharding import PartitionSpec as P

SG = 512
RADIX = 64
TS = 16
LONG = 4096
SUBS = 32
FACETS = 8
CAP = 4
LANES = 128
MESH = pl.DeviceIdType.MESH
F32 = jnp.float32
BF16 = jnp.bfloat16

kernel_width = 2.5
kernel_norm = 0.565


def as_real(theta):
    cosine, sine = np.cos(theta), np.sin(theta)
    return np.block([[cosine, sine], [-sine, cosine]])


def row_tables():
    idx = np.arange(RADIX)
    first = as_real(2 * np.pi * (np.outer(idx, idx) % RADIX) / RADIX)
    second = [
        as_real(2 * np.pi * (np.outer(k1 + RADIX * idx, idx) % LONG) / LONG) / RADIX
        for k1 in range(RADIX)
    ]
    return jnp.asarray(first, BF16), jnp.asarray(np.stack(second), BF16)


def col_tables():
    high = np.outer(np.arange(16), np.arange(LANES)) % LANES
    dense = as_real(2 * np.pi * high / LANES)
    low = 2 * np.pi * np.outer(np.arange(SUBS), np.arange(LANES)) / LONG
    twist = np.stack([np.cos(low), np.sin(low)]) / 64.0
    rep = np.zeros((512, 32))
    rep[np.arange(512), np.arange(512) // 16] = 1
    sel = np.zeros((2, 16, 16, 4, 2, 16))
    for z in range(2):
        for r in range(16):
            sel[z, :, r, :, z, r] = 1
    sel = sel.reshape(512, 128)
    keep = (np.arange(512)[:, None] % 16) == (np.arange(512)[None, :] // 16 % 16)
    return (
        jnp.asarray(dense, BF16),
        jnp.asarray(twist, F32),
        jnp.asarray(rep, BF16),
        jnp.asarray(rep.T, BF16),
        jnp.asarray(sel, BF16),
        jnp.asarray(keep, BF16),
    )


def mm(first, other):
    return jnp.dot(first, other, preferred_element_type=F32)


def mm_nt(first, other):
    return lax.dot_general(first, other, (((1,), (1,)), ((), ())), preferred_element_type=F32)


def mm_tn(first, other):
    return lax.dot_general(first, other, (((0,), (0,)), ((), ())), preferred_element_type=F32)


PITCH = RADIX + 1
WIDE = 2 * RADIX + 1


def strided(index, pitch):
    return pl.ds(index, RADIX, stride=pitch)


def transform_rows(fetch, mid_re, mid_im, first, second, put):
    def stage_a(step, carry):
        parts = []
        for u in range(2):
            real, imag = fetch(2 * step + u)
            parts.append(jnp.concatenate([real, imag], axis=0).astype(BF16))
        res = mm(first[...], jnp.concatenate(parts, axis=1))
        for u in range(2):
            rows = strided(2 * step + u, PITCH)
            mid_re[rows, :] = res[:RADIX, u * LANES : (u + 1) * LANES]
            mid_im[rows, :] = res[RADIX:, u * LANES : (u + 1) * LANES]
        return carry

    lax.fori_loop(0, RADIX // 2, stage_a, 0, unroll=8)

    def stage_b(step, carry):
        rows = pl.ds(step * PITCH, RADIX)
        block = jnp.concatenate([mid_re[rows, :], mid_im[rows, :]], axis=0).astype(BF16)
        res = mm(second[step], block)
        put(step, res[:RADIX], res[RADIX:])
        return carry

    lax.fori_loop(0, RADIX, stage_b, 0, unroll=16)


def forward_kernel(
    offs, turn, strip, row_win, col_win, first, second_hbm, out_hbm,
    re, im, mid_re, mid_im, wide_re, wide_im, second, out, second_sem, out_sem,
):
    table = pltpu.make_async_copy(second_hbm, second, second_sem)
    table.start()
    facet = lax.axis_index("facet")
    row_win = row_win[...].T
    scale = col_win[...]
    for block in range(RADIX):
        window = row_win[:, block : block + 1] * scale
        rows, src = pl.ds(block * PITCH, RADIX), pl.ds(block * RADIX, RADIX)
        re[rows, :] = strip[0, src, :].astype(F32) * window
        im[rows, :] = strip[1, src, :].astype(F32) * window
    table.wait()

    def fetch(index):
        rows = strided(index, PITCH)
        return re[rows, :], im[rows, :]

    def put(index, real, imag):
        here, before = strided(WIDE + index, WIDE), strided(RADIX + index, WIDE)
        wide_re[here, :] = real
        wide_im[here, :] = imag
        wide_re[before, :] = real
        wide_im[before, :] = imag

    transform_rows(fetch, mid_re, mid_im, first, second, put)

    def emit(which, carry):
        base = offs[which]
        index = (facet * base) & (FACETS - 1)
        cosine, sine = turn[0, index], turn[1, index]
        start = WIDE + base // RADIX * WIDE + base % RADIX
        for part in range(8):
            rows = pl.ds(start + part * WIDE, RADIX)
            real, imag = wide_re[rows, :], wide_im[rows, :]
            blocks = pl.ds(part * 4, 4)
            out[which, blocks, 0] = (cosine * real + sine * imag).astype(BF16).reshape(4, 16, LANES)
            out[which, blocks, 1] = (cosine * imag - sine * real).astype(BF16).reshape(4, 16, LANES)
        pltpu.make_async_copy(out.at[which], out_hbm.at[which], out_sem.at[which]).start()
        return carry

    lax.fori_loop(0, FACETS, emit, 0)
    for which in range(FACETS):
        pltpu.make_async_copy(out.at[which], out_hbm.at[which], out_sem.at[which]).wait()


def backward_kernel(
    offs, turn, strips, row_win, col_win, first, second_hbm, out_hbm,
    re, im, mid_re, mid_im, wide_re, wide_im, second, out, second_sem, out_sem,
):
    table = pltpu.make_async_copy(second_hbm, second, second_sem)
    table.start()
    facet = lax.axis_index("facet")
    row_win = row_win[...].T

    def clear(step, carry):
        rows = pl.ds(pl.multiple_of(step * 128, 128), 128)
        wide_re[rows, :] = jnp.zeros((128, LANES), F32)
        wide_im[rows, :] = jnp.zeros((128, LANES), F32)
        return carry

    lax.fori_loop(0, WIDE_ROWS // 128, clear, 0, unroll=2)

    def place(which, carry):
        base = offs[which]
        index = (facet * base) & (FACETS - 1)
        cosine, sine = turn[0, index], turn[1, index]
        start = WIDE + base // RADIX * WIDE + base % RADIX
        for part in range(8):
            rows = pl.ds(start + part * WIDE, RADIX)
            blocks = pl.ds(part * 4, 4)
            real = strips[which, blocks, 0].reshape(RADIX, LANES).astype(F32)
            imag = strips[which, blocks, 1].reshape(RADIX, LANES).astype(F32)
            wide_re[rows, :] = wide_re[rows, :] + (cosine * real - sine * imag)
            wide_im[rows, :] = wide_im[rows, :] - (sine * real + cosine * imag)
        return carry

    lax.fori_loop(0, FACETS, place, 0)
    table.wait()

    def fetch(index):
        here, before = strided(WIDE + index, WIDE), strided(RADIX + index, WIDE)
        return wide_re[here, :] + wide_re[before, :], wide_im[here, :] + wide_im[before, :]

    def put(index, real, imag):
        rows = strided(index, PITCH)
        re[rows, :] = real
        im[rows, :] = imag

    transform_rows(fetch, mid_re, mid_im, first, second, put)
    scale = col_win[...]
    quarter = LONG // 4
    copies = []
    for block in range(RADIX):
        window = row_win[:, block : block + 1] * scale
        rows, dst = pl.ds(block * PITCH, RADIX), pl.ds(block * RADIX, RADIX)
        out[0, dst, :] = (re[rows, :] * window).astype(BF16)
        out[1, dst, :] = (im[rows, :] * -window).astype(BF16)
        if block % 16 == 15:
            done = pl.ds(block // 16 * quarter, quarter)
            copies.append(
                pltpu.make_async_copy(out.at[:, done], out_hbm.at[:, done], out_sem.at[block // 16])
            )
            copies[-1].start()
    for copy in copies:
        copy.wait()


def times(pair, cosine, sine):
    return (pair[0] * cosine - pair[1] * sine, pair[0] * sine + pair[1] * cosine)


def times_unit(pair, num, den, sign):
    num = num % den
    if num == 0:
        return pair
    if 4 * num == den:
        return (-sign * pair[1], sign * pair[0])
    if 2 * num == den:
        return (-pair[0], -pair[1])
    angle = 2 * math.pi * num / den
    return times(pair, math.cos(angle), sign * math.sin(angle))


def small_dft(items, sign):
    count = len(items)
    if count == 1:
        return items
    even = small_dft(items[0::2], sign)
    odd = small_dft(items[1::2], sign)
    odd = [times_unit(odd[i], i, count, sign) for i in range(count // 2)]
    low = [(a[0] + b[0], a[1] + b[1]) for a, b in zip(even, odd)]
    high = [(a[0] - b[0], a[1] - b[1]) for a, b in zip(even, odd)]
    return low + high


def dft_over_blocks(get, put, work, sign):
    for lo in range(8):
        items = small_dft([get(lo + 8 * hi) for hi in range(4)], sign)
        for p_lo in range(4):
            value = times_unit(items[p_lo], lo * p_lo, SUBS, sign)
            work[p_lo * 8 + lo, 0] = value[0]
            work[p_lo * 8 + lo, 1] = value[1]
    for p_lo in range(4):
        items = small_dft([(work[p_lo * 8 + lo, 0], work[p_lo * 8 + lo, 1]) for lo in range(8)], sign)
        for p_hi in range(8):
            put(p_lo + 4 * p_hi, items[p_hi])


def columns_to_tiles(blocks, phase, dense, twist, rep, sel, keep, work, folded, tiles):
    def get(s):
        pair = (blocks[s, 0].astype(F32), blocks[s, 1].astype(F32))
        return times(pair, phase[0, s : s + 1, :], -phase[1, s : s + 1, :])

    def put(p, pair):
        pair = times(pair, twist[0, p : p + 1, :], -twist[1, p : p + 1, :])
        rows = slice(p * 16, p * 16 + 16)
        folded[rows, 0:LANES] = pair[0].astype(BF16)
        folded[rows, LANES : 2 * LANES] = pair[1].astype(BF16)

    dft_over_blocks(get, put, work, -1.0)
    flat = mm_nt(dense[...], folded[...]).astype(BF16)
    stacked = jnp.concatenate(
        [
            jnp.concatenate([flat[0:16, 0:256], flat[16:32, 0:256]], axis=1),
            jnp.concatenate([flat[0:16, 256:512], flat[16:32, 256:512]], axis=1),
        ],
        axis=0,
    )
    spread = mm(rep[...], stacked).astype(BF16) * keep[...]
    own = as_bf(iota((512, LANES), 1) // 32 == iota((512, LANES), 0) // TS % CAP)
    tiles[...] = mm(spread, sel[...]).astype(BF16) * own


def tiles_to_columns(tiles, phase, dense, twist, rep_t, sel, keep, work, folded_f32, images):
    spread = mm_nt(tiles[...], sel[...]).astype(BF16) * keep[...]
    stacked = mm(rep_t[...], spread).astype(BF16)
    flat = jnp.concatenate(
        [
            jnp.concatenate([stacked[0:16, 0:256], stacked[16:32, 0:256]], axis=1),
            jnp.concatenate([stacked[0:16, 256:512], stacked[16:32, 256:512]], axis=1),
        ],
        axis=0,
    )
    folded_f32[...] = mm_tn(flat, dense[...])

    def get(p):
        rows = slice(p * 16, p * 16 + 16)
        pair = (folded_f32[rows, 0:LANES], folded_f32[rows, LANES : 2 * LANES])
        return times(pair, twist[0, p : p + 1, :], twist[1, p : p + 1, :])

    def put(s, pair):
        pair = times(pair, phase[0, s : s + 1, :], phase[1, s : s + 1, :])
        images[s, 0] = pair[0].astype(BF16)
        images[s, 1] = pair[1].astype(BF16)

    dft_over_blocks(get, put, work, 1.0)


VALUES = 8


def unit_circle(turns, total):
    half = jnp.where(turns >= total / 2.0, turns - total, turns) * (math.pi / total)
    sq = half * half
    sine = 1.0 / 6227020800.0
    for term in (-1.0 / 39916800.0, 1.0 / 362880.0, -1.0 / 5040.0, 1.0 / 120.0, -1.0 / 6.0, 1.0):
        sine = sine * sq + term
    sine = sine * half
    cosine = 1.0 / 479001600.0
    for term in (-1.0 / 3628800.0, 1.0 / 40320.0, -1.0 / 720.0, 1.0 / 24.0, -0.5, 1.0):
        cosine = cosine * sq + term
    return 1.0 - 2.0 * sine * sine, 2.0 * sine * cosine


def over_pixels(values):
    return jnp.broadcast_to(values[:, None, :], (8, TS, LANES)).reshape(8 * TS, LANES)


def pack_visibilities(measured, masked, pixels, staged, packed):
    for part in range(4):
        rows = pl.ds(part * 32, 32)
        blocks = pl.ds(part * 8, 8)
        values = []
        for z in range(2):
            value = measured[rows, z, :]
            coarse = value.astype(BF16).astype(F32)
            values += [coarse, value - coarse]
        values.append(masked[rows, :])
        values += [pixels[rows, i, :].astype(F32) for i in range(3)]
        for q in range(VALUES):
            staged[blocks, q * CAP : (q + 1) * CAP, :] = values[q].reshape(8, CAP, LANES)
        packed[blocks] = staged[blocks].astype(BF16)


def visit(tiles, vis, my_tiles):
    pixel = (iota((8 * TS, LANES), 0) % TS).astype(F32)
    square = (pixel - 8.0) * (pixel - 8.0)
    own = (iota((64, LANES), 1) // 32 == iota((64, LANES), 0) // TS).astype(F32)

    for step in range(4):
        def value(q):
            return vis[q * SUBS + step * 8 : q * SUBS + step * 8 + 8, :]

        turns = over_pixels(value(7)) * square
        turns = turns - 256.0 * jnp.floor(turns * (1.0 / 256.0))
        cosine, sine = unit_circle(turns, 256.0)
        row_off = (pixel - over_pixels(value(5))) / kernel_width
        col_off = (pixel - over_pixels(value(6))) / kernel_width
        row_fall = kernel_norm * jnp.exp(-(row_off * row_off))
        col_fall = kernel_norm * jnp.exp(-(col_off * col_off))
        row_re, row_im = (row_fall * cosine).astype(BF16), (-row_fall * sine).astype(BF16)
        upper = jnp.concatenate([row_re, row_im], axis=1)
        lower = jnp.concatenate([-row_im, row_re], axis=1)
        weights = []
        for half in range(2):
            pieces = []
            for slot in range(4):
                src = slice(half * 64 + slot * TS, half * 64 + slot * TS + TS)
                pieces += [upper[src], lower[src]]
            weights.append(jnp.concatenate(pieces, axis=0))
        col_re = (col_fall * cosine).astype(BF16).astype(F32)
        col_im = (-col_fall * sine).astype(BF16).astype(F32)
        first = step * 128
        part = jnp.concatenate(
            [mm(tiles[first + half * 64 : first + half * 64 + 64, :], weights[half]) for half in range(2)],
            axis=0,
        )
        part_re, part_im = part[:, 0:LANES], part[:, LANES : 2 * LANES]
        pred_re = jnp.sum((col_re * part_re - col_im * part_im).reshape(8, TS, LANES), axis=1)
        pred_im = jnp.sum((col_re * part_im + col_im * part_re).reshape(8, TS, LANES), axis=1)
        weight = value(4)
        res_re = over_pixels(weight * (value(0) + value(1) - pred_re))
        res_im = over_pixels(weight * (value(2) + value(3) - pred_im))
        back_re = (col_re * res_re + col_im * res_im).astype(BF16)
        back_im = (col_re * res_im - col_im * res_re).astype(BF16)
        back = jnp.concatenate([back_re, back_im], axis=1)
        for half in range(2):
            grid = mm_nt(back[half * 64 : half * 64 + 64], weights[half]) * own
            my_tiles[first + half * 64 : first + half * 64 + 64, :] = grid.astype(BF16)


def as_bf(condition):
    return condition.astype(F32).astype(BF16)


def iota(shape, dim):
    return lax.broadcasted_iota(jnp.int32, shape, dim)


def masked_weights(weight, counts, masked):
    identity = as_bf(iota((LANES, LANES), 0) == iota((LANES, LANES), 1))
    spread = jnp.broadcast_to(counts[...].astype(F32), (LANES, LANES)).astype(BF16)
    column = mm_nt(identity, spread)
    masked[...] = jnp.where(iota((LANES, LANES), 1).astype(F32) < column, weight[...], 0.0)


def column_phase(facet, offsets, phase):
    mine = jnp.where(iota((1, FACETS), 1) == facet, offsets[...], 0)
    start = jnp.sum(mine.astype(F32), axis=1, keepdims=True).astype(jnp.int32)
    column = iota((SUBS, LANES), 0) * LANES + iota((SUBS, LANES), 1)
    turns = ((column * start) & (LONG - 1)).astype(F32)
    cosine, sine = unit_circle(turns, float(LONG))
    phase[0] = cosine
    phase[1] = sine


def routing(owners, choice):
    square = (SUBS, SUBS)
    up, across = iota(square, 0), iota(square, 1)
    named = as_bf(owners[...] == up)
    moved = as_bf(across == up % 2 * 16 + up // 2)
    identity = as_bf(up == across)
    earlier = mm(named, as_bf(up < across)).astype(BF16)
    named = mm(named, moved).astype(BF16)
    rank = jnp.sum(named.astype(F32) * mm(earlier, moved), axis=0, keepdims=True)
    rank = mm_nt(identity, jnp.broadcast_to(rank, (LANES, SUBS)).astype(BF16))
    by_tile = mm_nt(identity, named).astype(BF16)
    wide = (SUBS, SUBS * SUBS)
    by_tile = mm(by_tile, as_bf(iota(wide, 1) // SUBS == iota(wide, 0)))
    at_rank = (rank == (iota((SUBS, LANES), 1) % CAP).astype(F32)).astype(F32)
    both = by_tile * jnp.concatenate([at_rank] * 8, axis=1)
    which = iota(wide, 1) % SUBS // CAP
    for q in range(VALUES):
        choice[q * SUBS : (q + 1) * SUBS, :] = jnp.where(which == q, both, 0.0).astype(BF16)


def add_blocks(dst, sources, lo, count):
    def one(step, carry):
        total = sources[0][lo + step].astype(F32)
        for src in sources[1:]:
            total = total + src[lo + step].astype(F32)
        dst[lo + step] = total.astype(BF16)
        return carry

    lax.fori_loop(0, count, one, 0, unroll=4)


def middle_kernel(
    mine, offsets, owners, measured, weight, pixels, counts, dense, twist, rep, rep_t, sel, keep,
    out,
    pair_buf, sums, carry_a, carry_b, from_dn, from_up, total, gathered,
    work, folded, folded_f32, tiles, my_tiles, images,
    masked, phase, staged, packed, received, choice, vis,
    pair_s, pair_r, ring_s, ring_r, send_s, first_r, vis_r, image_r, gath_s, gath_r,
):
    me = lax.axis_index("sub")
    facet = lax.axis_index("facet")
    core, chip = lax.rem(facet, 2), facet // 2
    sib = facet + 1 - 2 * core
    up, dn = lax.rem(facet + 2, FACETS), lax.rem(facet + 6, FACETS)
    opp = lax.rem(facet + 4, FACETS)
    low, high = pl.ds(0, 16), pl.ds(16, 16)

    barrier = pltpu.get_barrier_semaphore()

    def greet(step, carry):
        pl.semaphore_signal(barrier, inc=1, device_id={"sub": lax.rem(me + step, SUBS)}, device_id_type=MESH)
        return carry

    for peer in (sib, up, dn):
        pl.semaphore_signal(barrier, inc=1, device_id={"facet": peer}, device_id_type=MESH)
    lax.fori_loop(1, SUBS, greet, 0)
    pl.semaphore_wait(barrier, SUBS + 2)

    def to_facet(src, dst, ssem, rsem, peer):
        return pltpu.make_async_remote_copy(
            src_ref=src, dst_ref=dst, send_sem=ssem, recv_sem=rsem,
            device_id={"facet": peer}, device_id_type=MESH,
        )

    def swap(src_of, dst, kind, rsem):
        def copy_to(peer, slot):
            return pltpu.make_async_remote_copy(
                src_ref=src_of.at[peer], dst_ref=dst.at[slot],
                send_sem=send_s.at[kind, peer], recv_sem=rsem.at[slot],
                device_id={"sub": peer}, device_id_type=MESH,
            )

        def send(step, carry):
            copy_to(lax.rem(me + step, SUBS), me).start()
            return carry

        def receive(step, carry):
            peer = lax.rem(me + SUBS - step, SUBS)
            copy_to(peer, peer).wait_recv()
            return carry

        def drain(step, carry):
            copy_to(lax.rem(me + step, SUBS), me).wait_send()
            return carry

        lax.fori_loop(1, SUBS, send, 0)
        dst[me] = src_of[me]
        return (
            lambda: lax.fori_loop(1, SUBS, receive, 0),
            lambda: lax.fori_loop(1, SUBS, drain, 0),
        )

    pairs = {}
    for hop in (2, 1, 3, 0):
        target = 2 * lax.rem(chip + hop, 4) + 1 - core
        pairs[hop] = to_facet(mine.at[target], pair_buf.at[hop], pair_s.at[hop], pair_r.at[hop], sib)
        pairs[hop].start()

    masked_weights(weight, counts, masked)
    pack_visibilities(measured, masked, pixels, staged, packed)
    receive_vis, drain_vis = swap(packed, received, 1, vis_r)

    def merge_pair(hop):
        pairs[hop].wait_recv()
        target = 2 * lax.rem(chip + hop, 4) + core
        add_blocks(sums.at[hop], [mine.at[target], pair_buf.at[hop]], 0, SUBS)

    merge_pair(2)
    ring = [
        to_facet(sums.at[2, low], carry_a, ring_s.at[0], ring_r.at[0], up),
        to_facet(sums.at[2, high], carry_b, ring_s.at[1], ring_r.at[1], dn),
        to_facet(sums.at[1, high], from_dn.at[high], ring_s.at[2], ring_r.at[2], up),
        to_facet(sums.at[3, low], from_up.at[low], ring_s.at[3], ring_r.at[3], dn),
        to_facet(sums.at[1, low], from_dn.at[low], ring_s.at[4], ring_r.at[4], up),
        to_facet(sums.at[3, high], from_up.at[high], ring_s.at[5], ring_r.at[5], dn),
    ]
    ring[0].start()
    ring[1].start()
    merge_pair(1)
    ring[2].start()
    merge_pair(3)
    ring[3].start()
    column_phase(facet, offsets, phase)
    routing(owners, choice)
    ring[0].wait_recv()
    add_blocks(sums.at[1, low], [sums.at[1, low], carry_a], 0, 16)
    ring[4].start()
    ring[1].wait_recv()
    add_blocks(sums.at[3, high], [sums.at[3, high], carry_b], 0, 16)
    ring[5].start()
    pairs[0].wait_recv()
    for step in (2, 3, 4, 5):
        ring[step].wait_recv()
    own_target = 2 * chip + core
    add_blocks(total, [mine.at[own_target], pair_buf.at[0], from_dn, from_up], 0, SUBS)

    receive_rows, drain_rows = swap(total, gathered, 0, first_r)
    receive_vis()
    vis[...] = mm(choice[...], received[...].reshape(SUBS * SUBS, LANES))
    receive_rows()
    columns_to_tiles(gathered, phase, dense, twist, rep, sel, keep, work, folded, tiles)
    visit(tiles, vis, my_tiles)
    tiles_to_columns(my_tiles, phase, dense, twist, rep_t, sel, keep, work, folded_f32, images)
    receive_images, drain_images = swap(images, out.at[facet], 2, image_r)
    receive_images()

    def share(index, src, peer):
        return to_facet(src, src, gath_s.at[index], gath_r.at[index], peer)

    own = out.at[facet]
    sends = [share(0, own, up), share(1, own, dn), share(2, own, sib)]
    for copy in sends:
        copy.start()

    def arrives(index, ref):
        share(index, ref, sib).wait_recv()

    arrives(0, out.at[dn])
    onward = [share(3, out.at[dn, low], up), share(5, out.at[dn], sib)]
    for copy in onward:
        copy.start()
    arrives(1, out.at[up])
    more = [share(4, out.at[up, high], dn), share(6, out.at[up], sib)]
    for copy in more:
        copy.start()
    arrives(3, out.at[opp, low])
    last = [share(7, out.at[opp, low], sib)]
    last[0].start()
    arrives(4, out.at[opp, high])
    last.append(share(8, out.at[opp, high], sib))
    last[1].start()
    other = 1 - 2 * core
    arrives(2, out.at[sib])
    arrives(5, out.at[dn + other])
    arrives(6, out.at[up + other])
    arrives(7, out.at[opp + other, low])
    arrives(8, out.at[opp + other, high])
    for copy in sends + onward + more + last + ring:
        copy.wait_send()
    for hop in range(4):
        pairs[hop].wait_send()
    for drain in (drain_rows, drain_vis, drain_images):
        drain()


def vmem_specs(count):
    return [pl.BlockSpec(memory_space=pltpu.VMEM)] * count


def smem_specs(count):
    return [pl.BlockSpec(memory_space=pltpu.SMEM)] * count


BIG = 60 * 1024 * 1024
STRIPS = (FACETS, SUBS, 2, 16, LANES)
WIDE_ROWS = 66 * 128


def rows_call(body, shape):
    narrow, wide = pltpu.VMEM((RADIX * PITCH, LANES), F32), pltpu.VMEM((WIDE_ROWS, LANES), F32)
    return pl.pallas_call(
        body,
        out_shape=jax.ShapeDtypeStruct(shape, BF16),
        in_specs=smem_specs(2) + vmem_specs(4) + [pl.BlockSpec(memory_space=pl.ANY)],
        out_specs=pl.BlockSpec(memory_space=pl.ANY),
        scratch_shapes=[narrow] * 4
        + [wide] * 2
        + [
            pltpu.VMEM((RADIX, 2 * RADIX, 2 * RADIX), BF16),
            pltpu.VMEM(shape, BF16),
            pltpu.SemaphoreType.DMA,
            pltpu.SemaphoreType.DMA((FACETS,)),
        ],
        compiler_params=pltpu.CompilerParams(vmem_limit_bytes=BIG),
    )


def middle_call():
    block = (SUBS, 2, 16, LANES)
    half = (16, 2, 16, LANES)
    values = (SUBS, VALUES * CAP, LANES)
    vm = pltpu.VMEM
    dma = pltpu.SemaphoreType.DMA
    return pl.pallas_call(
        middle_kernel,
        out_shape=jax.ShapeDtypeStruct(STRIPS, BF16),
        in_specs=vmem_specs(13),
        out_specs=pl.BlockSpec(memory_space=pltpu.VMEM),
        scratch_shapes=[
            vm((4,) + block, BF16), vm((4,) + block, BF16), vm(half, BF16), vm(half, BF16),
            vm(block, BF16), vm(block, BF16), vm(block, BF16), vm(block, BF16),
            vm(block, F32), vm((512, 256), BF16), vm((512, 256), F32),
            vm((512, LANES), BF16), vm((512, LANES), BF16), vm(block, BF16),
            vm((LANES, LANES), F32), vm((2, SUBS, LANES), F32),
            vm(values, F32), vm(values, BF16), vm(values, BF16),
            vm((VALUES * SUBS, SUBS * SUBS), BF16), vm((VALUES * SUBS, LANES), F32),
            dma((4,)), dma((4,)), dma((6,)), dma((6,)), dma((3, SUBS)),
            dma((SUBS,)), dma((SUBS,)), dma((SUBS,)), dma((9,)), dma((9,)),
        ],
        compiler_params=pltpu.CompilerParams(
            vmem_limit_bytes=BIG, collective_id=0, has_side_effects=True
        ),
    )


def per_device(
    facet_strips, row_window, col_window, row_offsets, col_offsets,
    tile_owner, measured, vis_weight, uvw_pixels, vis_count,
):
    first, second = row_tables()
    dense, twist, rep, rep_t, sel, keep = col_tables()
    eighth = 2 * np.pi * np.arange(FACETS) / FACETS
    turn = jnp.asarray(np.stack([np.cos(eighth), np.sin(eighth)]), F32)
    row_win = row_window.reshape(RADIX, RADIX)
    col_win = col_window.reshape(1, LANES)
    contributions = rows_call(forward_kernel, STRIPS)(
        row_offsets, turn, facet_strips, row_win, col_win, first, second
    )
    strips = middle_call()(
        contributions, col_offsets.reshape(1, FACETS), tile_owner.reshape(1, SUBS), measured[0, 0],
        vis_weight[0, 0], uvw_pixels[0, 0], vis_count.reshape(1, LANES),
        dense, twist, rep, rep_t, sel, keep,
    )
    return rows_call(backward_kernel, facet_strips.shape)(
        row_offsets, turn, strips, row_win, col_win, first, second
    )


def solution(mesh):
    in_specs = (
        P(None, "facet", "sub"),
        P(),
        P("sub"),
        P(),
        P(),
        P("sub", "facet", None, None),
        P("facet", "sub", None, None, None),
        P("facet", "sub", None, None),
        P("facet", "sub", None, None, None),
        P("facet", "sub", None),
    )
    return jax.shard_map(
        per_device, mesh=mesh, in_specs=in_specs, out_specs=P(None, "facet", "sub"), check_vma=False
    )
```

time: 132 us -> 82.4 us (0.62)
  Pallas kernels: 117 us -> 78.9 us
  other arithmetic: 9.51 us -> 0 us
  local copies, waits for them, and re-layouts: 5.21 us -> 3.17 us
    pallas_call x2, Pallas kernels: 34.5 us -> 14.3 us  [the longest x1 7.22 us: per_device(): rows_call(backward_kernel, facet_strips.shape)]
    pallas_call x1, Pallas kernels: 82.1 us -> 64.7 us  [per_device(): middle_call()]
    unnamed x2 -> x0, other arithmetic: 2.24 us -> none
    mul x1 -> x0, other arithmetic: 1.95 us -> none  [per_device(): win = row_window[:, None] * col_window[None, :]]
    another operation x3 -> x0, other arithmetic: 1.93 us -> none  [the longest x2 1.32 us: per_device(): turn = jnp.stack([jnp.cos(turns), jnp.sin(turns)])]
    convert_element_type x2 -> x0, other arithmetic: 1.74 us -> none  [the longest x1 0.94 us: per_device(): pixels = uvw_pixels[0, 0].astype(F32)]
    broadcast_in_dim x5 -> x0, local copies, waits for them, and re-layouts: 1.71 us -> none  [the longest x1 0.86 us: route_tables(): jnp.broadcast_to(owners[:, None], (512, LANES))]
where the time goes in v1:
time: 82.4 us; the launch traced here: 82.1 us
  Pallas kernels  78.9 us (96%)
  local copies, waits for them, and re-layouts  3.17 us (4%)
    pallas_call x1, Pallas kernels, per_device(): middle_call()  64.7 us
    pallas_call x1, Pallas kernels, per_device(): rows_call(backward_kernel, facet_strips.shape)  7.22 us
    pallas_call x1, Pallas kernels, per_device(): rows_call(forward_kernel, STRIPS)  7.05 us
    unnamed x1, local copies, waits for them, and re-layouts  1.79 us

profile of v1, /device:TPU:1, one launch (start us, length us, event | category | flops | bytes accessed | tf_op | source)
XLA Modules:
  0.0 82.1 jit_solution(10323809710680326316)
XLA Ops:
  0.0 1.4 %reshape.15.row_win = f32[64,64]{1,0:T(8,128)} reshape(f32[4096]{0:T(1024)} %param.20) | data formatting | bytes 32768 | tf_op jit(solution)/shard_map/reshape | solution.py:672
  1.4 1.8 %copy.22 = s32[1,1,128,3,128]{4,3,2,1,0:T(4,128)} copy(s32[1,1,128,3,128]{4,2,3,1,0:T(8,128)} %param.27) | data formatting | bytes 393216 | tf_op args[8]
  3.2 7.1 %shard_map.181.mine = bf16[8,32,2,16,128]{4,3,2,1,0:T(8,128)(2,1)} custom-call(s32[8]{0:T(128)} %offs.3, f32[2,8]{1,0:T(2,128)} %constant.26.clone.turn, bf16[2,4096,128]{2,1,0:T(8,128)(2,1)} %strip.1, f32[64,64]{1,0:T(8,128)} %reshape.15.row_win, f32[1,128]{1,0:T(1,128)} %bitcast.12, bf16[128,128]{1,0:T(8,128)(2,1)} %constant.18.clone.first, ...), custom_call_target="tpu_custom_call" | custom-call | tf_op jit(solution)/shard_map/pallas_call | solution.py:674
  10.2 64.7 %shard_map.182.strips = bf16[8,32,2,16,128]{4,3,2,1,0:T(8,128)(2,1)} custom-call(bf16[8,32,2,16,128]{4,3,2,1,0:T(8,128)(2,1)} %shard_map.181.mine, s32[1,8]{1,0:T(1,128)} %bitcast.14, s32[1,32]{1,0:T(1,128)} %bitcast.15, f32[128,2,128]{2,1,0:T(2,128)} %bitcast.10, f32[128,128]{1,0:T(8,128)} %bitcast.11, s32[128,3,128]{2,1,0:T(4,128)} %bitcast.9, ...), custom_call_target="tpu_custom_call" | custom-call | tf_op jit(solution)/shard_map/pallas_call | solution.py:677
  74.9 7.2 %shard_map.183 = bf16[2,4096,128]{2,1,0:T(8,128)(2,1)} custom-call(s32[8]{0:T(128)} %offs.3, f32[2,8]{1,0:T(2,128)} %constant.26.clone.turn, bf16[8,32,2,16,128]{4,3,2,1,0:T(8,128)(2,1)} %shard_map.182.strips, f32[64,64]{1,0:T(8,128)} %reshape.15.row_win, f32[1,128]{1,0:T(1,128)} %bitcast.13, bf16[128,128]{1,0:T(8,128)(2,1)} %constant.18.clone.first, ...), custom_call_target="tpu_custom_call" | custom-call | tf_op jit(solution)/shard_map/pallas_call | solution.py:682

commit v2 on v1

--- a/solution.py
+++ b/solution.py
@@ -107,22 +107,19 @@
     lax.fori_loop(0, RADIX, stage_b, 0, unroll=16)
 
 
-def forward_kernel(
-    offs, turn, strip, row_win, col_win, first, second_hbm, out_hbm,
-    re, im, mid_re, mid_im, wide_re, wide_im, second, out, second_sem, out_sem,
-):
-    table = pltpu.make_async_copy(second_hbm, second, second_sem)
-    table.start()
-    facet = lax.axis_index("facet")
-    row_win = row_win[...].T
-    scale = col_win[...]
+def load_strip(strip, row_win, col_win, loads, re, im):
+    row_win, scale = row_win[...].T, col_win[...]
     for block in range(RADIX):
-        window = row_win[:, block : block + 1] * scale
+        if block % (RADIX // len(loads)) == 0:
+            loads[block * len(loads) // RADIX].wait()
+        half = block % 2 * RADIX
+        window = row_win[half : half + RADIX, block // 2 : block // 2 + 1] * scale
         rows, src = pl.ds(block * PITCH, RADIX), pl.ds(block * RADIX, RADIX)
         re[rows, :] = strip[0, src, :].astype(F32) * window
         im[rows, :] = strip[1, src, :].astype(F32) * window
-    table.wait()
-
+
+
+def spectrum(re, im, mid_re, mid_im, wide_re, wide_im, first, second):
     def fetch(index):
         rows = strided(index, PITCH)
         return re[rows, :], im[rows, :]
@@ -136,29 +133,29 @@
 
     transform_rows(fetch, mid_re, mid_im, first, second, put)
 
-    def emit(which, carry):
-        base = offs[which]
-        index = (facet * base) & (FACETS - 1)
-        cosine, sine = turn[0, index], turn[1, index]
-        start = WIDE + base // RADIX * WIDE + base % RADIX
-        for part in range(8):
-            rows = pl.ds(start + part * WIDE, RADIX)
-            real, imag = wide_re[rows, :], wide_im[rows, :]
-            blocks = pl.ds(part * 4, 4)
-            out[which, blocks, 0] = (cosine * real + sine * imag).astype(BF16).reshape(4, 16, LANES)
-            out[which, blocks, 1] = (cosine * imag - sine * real).astype(BF16).reshape(4, 16, LANES)
-        pltpu.make_async_copy(out.at[which], out_hbm.at[which], out_sem.at[which]).start()
-        return carry
-
-    lax.fori_loop(0, FACETS, emit, 0)
+
+def cut_rows(which, facet, offs, turn, wide_re, wide_im, out):
+    base = offs[which]
+    index = (facet * base) & (FACETS - 1)
+    cosine, sine = turn[0, index], turn[1, index]
+    start = WIDE + base // RADIX * WIDE + base % RADIX
+    for part in range(8):
+        rows = pl.ds(start + part * WIDE, RADIX)
+        real, imag = wide_re[rows, :], wide_im[rows, :]
+        blocks = pl.ds(part * 4, 4)
+        out[which, blocks, 0] = (cosine * real + sine * imag).astype(BF16).reshape(4, 16, LANES)
+        out[which, blocks, 1] = (cosine * imag - sine * real).astype(BF16).reshape(4, 16, LANES)
+
+
+def backward_kernel(
+    offs, turn, row_win, col_win, first, strips_hbm, second_hbm, out_hbm,
+    re, im, mid_re, mid_im, wide_re, wide_im, strips, second, out, second_sem, strip_sem, out_sem,
+):
+    def load(which):
+        return pltpu.make_async_copy(strips_hbm.at[which], strips.at[which], strip_sem.at[which])
+
     for which in range(FACETS):
-        pltpu.make_async_copy(out.at[which], out_hbm.at[which], out_sem.at[which]).wait()
-
-
-def backward_kernel(
-    offs, turn, strips, row_win, col_win, first, second_hbm, out_hbm,
-    re, im, mid_re, mid_im, wide_re, wide_im, second, out, second_sem, out_sem,
-):
+        load(which).start()
     table = pltpu.make_async_copy(second_hbm, second, second_sem)
     table.start()
     facet = lax.axis_index("facet")
@@ -173,6 +170,7 @@
     lax.fori_loop(0, WIDE_ROWS // 128, clear, 0, unroll=2)
 
     def place(which, carry):
+        load(which).wait()
         base = offs[which]
         index = (facet * base) & (FACETS - 1)
         cosine, sine = turn[0, index], turn[1, index]
@@ -203,7 +201,8 @@
     quarter = LONG // 4
     copies = []
     for block in range(RADIX):
-        window = row_win[:, block : block + 1] * scale
+        half = block % 2 * RADIX
+        window = row_win[half : half + RADIX, block // 2 : block // 2 + 1] * scale
         rows, dst = pl.ds(block * PITCH, RADIX), pl.ds(block * RADIX, RADIX)
         out[0, dst, :] = (re[rows, :] * window).astype(BF16)
         out[1, dst, :] = (im[rows, :] * -window).astype(BF16)
@@ -338,7 +337,7 @@
             coarse = value.astype(BF16).astype(F32)
             values += [coarse, value - coarse]
         values.append(masked[rows, :])
-        values += [pixels[rows, i, :].astype(F32) for i in range(3)]
+        values += [pixels[i, rows, :].astype(F32) for i in range(3)]
         for q in range(VALUES):
             staged[blocks, q * CAP : (q + 1) * CAP, :] = values[q].reshape(8, CAP, LANES)
         packed[blocks] = staged[blocks].astype(BF16)
@@ -447,12 +446,15 @@
     lax.fori_loop(0, count, one, 0, unroll=4)
 
 
-def middle_kernel(
-    mine, offsets, owners, measured, weight, pixels, counts, dense, twist, rep, rep_t, sel, keep,
-    out,
+def facet_to_strips_kernel(
+    offs, turn, row_win, col_win, first, offsets, owners, measured, weight, pixels, counts,
+    dense, twist, rep, rep_t, sel, strip_hbm, second_hbm, keep_hbm,
+    out_hbm,
+    strip, re, im, mid_re, mid_im, wide_re, wide_im, second, keep, mine,
     pair_buf, sums, carry_a, carry_b, from_dn, from_up, total, gathered,
-    work, folded, folded_f32, tiles, my_tiles, images,
+    work, folded, folded_f32, tiles, my_tiles, images, out,
     masked, phase, staged, packed, received, choice, vis,
+    load_sem, out_sem,
     pair_s, pair_r, ring_s, ring_r, send_s, first_r, vis_r, image_r, gath_s, gath_r,
 ):
     me = lax.axis_index("sub")
@@ -472,6 +474,22 @@
     for peer in (sib, up, dn):
         pl.semaphore_signal(barrier, inc=1, device_id={"facet": peer}, device_id_type=MESH)
     lax.fori_loop(1, SUBS, greet, 0)
+    quarter = LONG // 4
+    loads = [
+        pltpu.make_async_copy(
+            strip_hbm.at[:, pl.ds(i * quarter, quarter)], strip.at[:, pl.ds(i * quarter, quarter)], load_sem.at[i]
+        )
+        for i in range(4)
+    ]
+    second_load = pltpu.make_async_copy(second_hbm, second, load_sem.at[4])
+    keep_load = pltpu.make_async_copy(keep_hbm, keep, load_sem.at[5])
+    for copy in loads + [second_load, keep_load]:
+        copy.start()
+    masked_weights(weight, counts, masked)
+    pack_visibilities(measured, masked, pixels, staged, packed)
+    load_strip(strip, row_win, col_win, loads, re, im)
+    second_load.wait()
+    spectrum(re, im, mid_re, mid_im, wide_re, wide_im, first, second)
     pl.semaphore_wait(barrier, SUBS + 2)
 
     def to_facet(src, dst, ssem, rsem, peer):
@@ -508,15 +526,16 @@
             lambda: lax.fori_loop(1, SUBS, drain, 0),
         )
 
+    receive_vis, drain_vis = swap(packed, received, 1, vis_r)
+
     pairs = {}
     for hop in (2, 1, 3, 0):
         target = 2 * lax.rem(chip + hop, 4) + 1 - core
+        cut_rows(target, facet, offs, turn, wide_re, wide_im, mine)
         pairs[hop] = to_facet(mine.at[target], pair_buf.at[hop], pair_s.at[hop], pair_r.at[hop], sib)
         pairs[hop].start()
-
-    masked_weights(weight, counts, masked)
-    pack_visibilities(measured, masked, pixels, staged, packed)
-    receive_vis, drain_vis = swap(packed, received, 1, vis_r)
+    for hop in (2, 1, 3, 0):
+        cut_rows(2 * lax.rem(chip + hop, 4) + core, facet, offs, turn, wide_re, wide_im, mine)
 
     def merge_pair(hop):
         pairs[hop].wait_recv()
@@ -553,6 +572,7 @@
     add_blocks(total, [mine.at[own_target], pair_buf.at[0], from_dn, from_up], 0, SUBS)
 
     receive_rows, drain_rows = swap(total, gathered, 0, first_r)
+    keep_load.wait()
     receive_vis()
     vis[...] = mm(choice[...], received[...].reshape(SUBS * SUBS, LANES))
     receive_rows()
@@ -565,40 +585,59 @@
     def share(index, src, peer):
         return to_facet(src, src, gath_s.at[index], gath_r.at[index], peer)
 
+    stores = []
+
+    def store(ref_of):
+        copy = pltpu.make_async_copy(ref_of(out), ref_of(out_hbm), out_sem.at[len(stores)])
+        copy.start()
+        stores.append(copy)
+
+    def whole(which):
+        return lambda ref: ref.at[which]
+
+    def part(which, rows):
+        return lambda ref: ref.at[which, rows]
+
     own = out.at[facet]
     sends = [share(0, own, up), share(1, own, dn), share(2, own, sib)]
     for copy in sends:
         copy.start()
-
-    def arrives(index, ref):
-        share(index, ref, sib).wait_recv()
-
-    arrives(0, out.at[dn])
-    onward = [share(3, out.at[dn, low], up), share(5, out.at[dn], sib)]
-    for copy in onward:
-        copy.start()
-    arrives(1, out.at[up])
-    more = [share(4, out.at[up, high], dn), share(6, out.at[up], sib)]
-    for copy in more:
-        copy.start()
-    arrives(3, out.at[opp, low])
-    last = [share(7, out.at[opp, low], sib)]
-    last[0].start()
-    arrives(4, out.at[opp, high])
-    last.append(share(8, out.at[opp, high], sib))
-    last[1].start()
+    store(whole(facet))
+
+    def arrives(index, ref_of):
+        share(index, ref_of(out), sib).wait_recv()
+        store(ref_of)
+
+    def forward(index, ref, peer):
+        sends.append(share(index, ref, peer))
+        sends[-1].start()
+
+    share(0, out.at[dn], sib).wait_recv()
+    forward(3, out.at[dn, low], up)
+    forward(5, out.at[dn], sib)
+    store(whole(dn))
+    share(1, out.at[up], sib).wait_recv()
+    forward(4, out.at[up, high], dn)
+    forward(6, out.at[up], sib)
+    store(whole(up))
     other = 1 - 2 * core
-    arrives(2, out.at[sib])
-    arrives(5, out.at[dn + other])
-    arrives(6, out.at[up + other])
-    arrives(7, out.at[opp + other, low])
-    arrives(8, out.at[opp + other, high])
-    for copy in sends + onward + more + last + ring:
+    arrives(2, whole(sib))
+    arrives(5, whole(dn + other))
+    arrives(6, whole(up + other))
+    share(3, out.at[opp, low], sib).wait_recv()
+    forward(7, out.at[opp, low], sib)
+    store(part(opp, low))
+    share(4, out.at[opp, high], sib).wait_recv()
+    forward(8, out.at[opp, high], sib)
+    store(part(opp, high))
+    arrives(7, part(opp + other, low))
+    arrives(8, part(opp + other, high))
+    for copy in sends + ring + list(pairs.values()):
         copy.wait_send()
-    for hop in range(4):
-        pairs[hop].wait_send()
     for drain in (drain_rows, drain_vis, drain_images):
         drain()
+    for copy in stores:
+        copy.wait()
 
 
 def vmem_specs(count):
@@ -614,44 +653,60 @@
 WIDE_ROWS = 66 * 128
 
 
-def rows_call(body, shape):
+def any_specs(count):
+    return [pl.BlockSpec(memory_space=pl.ANY)] * count
+
+
+def row_scratch():
     narrow, wide = pltpu.VMEM((RADIX * PITCH, LANES), F32), pltpu.VMEM((WIDE_ROWS, LANES), F32)
+    return [narrow] * 4 + [wide] * 2
+
+
+TABLE = (RADIX, 2 * RADIX, 2 * RADIX)
+
+
+def backward_call(shape):
     return pl.pallas_call(
-        body,
+        backward_kernel,
         out_shape=jax.ShapeDtypeStruct(shape, BF16),
-        in_specs=smem_specs(2) + vmem_specs(4) + [pl.BlockSpec(memory_space=pl.ANY)],
+        in_specs=smem_specs(2) + vmem_specs(3) + any_specs(2),
         out_specs=pl.BlockSpec(memory_space=pl.ANY),
-        scratch_shapes=[narrow] * 4
-        + [wide] * 2
+        scratch_shapes=row_scratch()
         + [
-            pltpu.VMEM((RADIX, 2 * RADIX, 2 * RADIX), BF16),
+            pltpu.VMEM(STRIPS, BF16),
+            pltpu.VMEM(TABLE, BF16),
             pltpu.VMEM(shape, BF16),
             pltpu.SemaphoreType.DMA,
             pltpu.SemaphoreType.DMA((FACETS,)),
+            pltpu.SemaphoreType.DMA((4,)),
         ],
         compiler_params=pltpu.CompilerParams(vmem_limit_bytes=BIG),
     )
 
 
-def middle_call():
+def strips_call(shape):
     block = (SUBS, 2, 16, LANES)
     half = (16, 2, 16, LANES)
     values = (SUBS, VALUES * CAP, LANES)
     vm = pltpu.VMEM
     dma = pltpu.SemaphoreType.DMA
     return pl.pallas_call(
-        middle_kernel,
+        facet_to_strips_kernel,
         out_shape=jax.ShapeDtypeStruct(STRIPS, BF16),
-        in_specs=vmem_specs(13),
-        out_specs=pl.BlockSpec(memory_space=pltpu.VMEM),
-        scratch_shapes=[
+        in_specs=smem_specs(2) + vmem_specs(14) + any_specs(3),
+        out_specs=pl.BlockSpec(memory_space=pl.ANY),
+        scratch_shapes=[vm(shape, BF16)]
+        + row_scratch()
+        + [
+            vm(TABLE, BF16), vm((512, 512), BF16), vm(STRIPS, BF16),
             vm((4,) + block, BF16), vm((4,) + block, BF16), vm(half, BF16), vm(half, BF16),
             vm(block, BF16), vm(block, BF16), vm(block, BF16), vm(block, BF16),
             vm(block, F32), vm((512, 256), BF16), vm((512, 256), F32),
-            vm((512, LANES), BF16), vm((512, LANES), BF16), vm(block, BF16),
+            vm((512, LANES), BF16), vm((512, LANES), BF16), vm(block, BF16), vm(STRIPS, BF16),
             vm((LANES, LANES), F32), vm((2, SUBS, LANES), F32),
             vm(values, F32), vm(values, BF16), vm(values, BF16),
             vm((VALUES * SUBS, SUBS * SUBS), BF16), vm((VALUES * SUBS, LANES), F32),
+            dma((6,)), dma((10,)),
             dma((4,)), dma((4,)), dma((6,)), dma((6,)), dma((3, SUBS)),
             dma((SUBS,)), dma((SUBS,)), dma((SUBS,)), dma((9,)), dma((9,)),
         ],
@@ -669,18 +724,16 @@
     dense, twist, rep, rep_t, sel, keep = col_tables()
     eighth = 2 * np.pi * np.arange(FACETS) / FACETS
     turn = jnp.asarray(np.stack([np.cos(eighth), np.sin(eighth)]), F32)
-    row_win = row_window.reshape(RADIX, RADIX)
+    row_win = row_window.reshape(LONG // LANES, LANES)
     col_win = col_window.reshape(1, LANES)
-    contributions = rows_call(forward_kernel, STRIPS)(
-        row_offsets, turn, facet_strips, row_win, col_win, first, second
-    )
-    strips = middle_call()(
-        contributions, col_offsets.reshape(1, FACETS), tile_owner.reshape(1, SUBS), measured[0, 0],
-        vis_weight[0, 0], uvw_pixels[0, 0], vis_count.reshape(1, LANES),
-        dense, twist, rep, rep_t, sel, keep,
-    )
-    return rows_call(backward_kernel, facet_strips.shape)(
-        row_offsets, turn, strips, row_win, col_win, first, second
+    strips = strips_call(facet_strips.shape)(
+        row_offsets, turn, row_win, col_win, first,
+        col_offsets.reshape(1, FACETS), tile_owner.reshape(1, SUBS), measured[0, 0],
+        vis_weight[0, 0], jnp.transpose(uvw_pixels[0, 0], (1, 0, 2)), vis_count.reshape(1, LANES),
+        dense, twist, rep, rep_t, sel, facet_strips, second, keep,
+    )
+    return backward_call(facet_strips.shape)(
+        row_offsets, turn, row_win, col_win, first, strips, second
     )
 
 

time: 82.4 us -> 69.9 us (0.85)
  Pallas kernels: 78.9 us -> 69.8 us
  local copies, waits for them, and re-layouts: 3.17 us -> 0 us
    pallas_call x3 -> x2, Pallas kernels: 78.9 us -> 69.8 us  [the longest x1 62.6 us: per_device(): strips_call(facet_strips.shape)]
    unnamed x1 -> x0, local copies, waits for them, and re-layouts: 1.79 us -> none
    reshape x1 -> x0, local copies, waits for them, and re-layouts: 1.39 us -> none  [per_device(): row_win = row_window.reshape(RADIX, RADIX)]
where the time goes in v2:
time: 69.9 us; the launch traced here: 69.8 us
  Pallas kernels  69.8 us (100%)
    pallas_call x1, Pallas kernels, per_device(): strips_call(facet_strips.shape)  62.6 us
    pallas_call x1, Pallas kernels, per_device(): backward_call(facet_strips.shape)  7.11 us

profile of v2, /device:TPU:1, one launch (start us, length us, event | category | flops | bytes accessed | tf_op | source)
XLA Modules:
  0.0 69.8 jit_solution(13185157879452914305)
XLA Ops:
  0.0 62.6 %shard_map.181.strips_hbm = bf16[8,32,2,16,128]{4,3,2,1,0:T(8,128)(2,1)} custom-call(s32[8]{0:T(128)} %offs.3, f32[2,8]{1,0:T(2,128)} %constant.26.clone.turn, f32[32,128]{1,0:T(8,128)} %bitcast.13, f32[1,128]{1,0:T(1,128)} %bitcast.15, bf16[128,128]{1,0:T(8,128)(2,1)} %constant.18.clone.first, s32[1,8]{1,0:T(1,128)} %bitcast.17, s32[1,32]{1,0:T(1,128)} %bitcast.18, ...), custom_call_target="tpu_custom_call" | custom-call | tf_op jit(solution)/shard_map/pallas_call | solution.py:729
  62.7 7.1 %shard_map.182 = bf16[2,4096,128]{2,1,0:T(8,128)(2,1)} custom-call(s32[8]{0:T(128)} %offs.3, f32[2,8]{1,0:T(2,128)} %constant.26.clone.turn, f32[32,128]{1,0:T(8,128)} %bitcast.14, f32[1,128]{1,0:T(1,128)} %bitcast.16, bf16[128,128]{1,0:T(8,128)(2,1)} %constant.18.clone.first, bf16[8,32,2,16,128]{4,3,2,1,0:T(8,128)(2,1)} %shard_map.181.strips_hbm, ...), custom_call_target="tpu_custom_call" | custom-call | tf_op jit(solution)/shard_map/pallas_call | solution.py:735

commit v3 on v2

--- a/solution.py
+++ b/solution.py
@@ -143,8 +143,8 @@
         rows = pl.ds(start + part * WIDE, RADIX)
         real, imag = wide_re[rows, :], wide_im[rows, :]
         blocks = pl.ds(part * 4, 4)
-        out[which, blocks, 0] = (cosine * real + sine * imag).astype(BF16).reshape(4, 16, LANES)
-        out[which, blocks, 1] = (cosine * imag - sine * real).astype(BF16).reshape(4, 16, LANES)
+        out[which, 0, blocks] = (cosine * real + sine * imag).astype(BF16).reshape(4, 16, LANES)
+        out[which, 1, blocks] = (cosine * imag - sine * real).astype(BF16).reshape(4, 16, LANES)
 
 
 def backward_kernel(
@@ -178,8 +178,8 @@
         for part in range(8):
             rows = pl.ds(start + part * WIDE, RADIX)
             blocks = pl.ds(part * 4, 4)
-            real = strips[which, blocks, 0].reshape(RADIX, LANES).astype(F32)
-            imag = strips[which, blocks, 1].reshape(RADIX, LANES).astype(F32)
+            real = strips[which, 0, blocks].reshape(RADIX, LANES).astype(F32)
+            imag = strips[which, 1, blocks].reshape(RADIX, LANES).astype(F32)
             wide_re[rows, :] = wide_re[rows, :] + (cosine * real - sine * imag)
             wide_im[rows, :] = wide_im[rows, :] - (sine * real + cosine * imag)
         return carry
@@ -259,7 +259,7 @@
 
 def columns_to_tiles(blocks, phase, dense, twist, rep, sel, keep, work, folded, tiles):
     def get(s):
-        pair = (blocks[s, 0].astype(F32), blocks[s, 1].astype(F32))
+        pair = (blocks[0, s].astype(F32), blocks[1, s].astype(F32))
         return times(pair, phase[0, s : s + 1, :], -phase[1, s : s + 1, :])
 
     def put(p, pair):
@@ -301,8 +301,8 @@
 
     def put(s, pair):
         pair = times(pair, phase[0, s : s + 1, :], phase[1, s : s + 1, :])
-        images[s, 0] = pair[0].astype(BF16)
-        images[s, 1] = pair[1].astype(BF16)
+        images[0, s] = pair[0].astype(BF16)
+        images[1, s] = pair[1].astype(BF16)
 
     dft_over_blocks(get, put, work, 1.0)
 
@@ -455,7 +455,7 @@
     work, folded, folded_f32, tiles, my_tiles, images, out,
     masked, phase, staged, packed, received, choice, vis,
     load_sem, out_sem,
-    pair_s, pair_r, ring_s, ring_r, send_s, first_r, vis_r, image_r, gath_s, gath_r,
+    pair_s, pair_r, ring_s, ring_r, send_s, rows_r, vis_r, image_r, gath_s, gath_r,
 ):
     me = lax.axis_index("sub")
     facet = lax.axis_index("facet")
@@ -526,115 +526,153 @@
             lambda: lax.fori_loop(1, SUBS, drain, 0),
         )
 
-    receive_vis, drain_vis = swap(packed, received, 1, vis_r)
-
     pairs = {}
-    for hop in (2, 1, 3, 0):
-        target = 2 * lax.rem(chip + hop, 4) + 1 - core
-        cut_rows(target, facet, offs, turn, wide_re, wide_im, mine)
-        pairs[hop] = to_facet(mine.at[target], pair_buf.at[hop], pair_s.at[hop], pair_r.at[hop], sib)
-        pairs[hop].start()
-    for hop in (2, 1, 3, 0):
-        cut_rows(2 * lax.rem(chip + hop, 4) + core, facet, offs, turn, wide_re, wide_im, mine)
-
-    def merge_pair(hop):
-        pairs[hop].wait_recv()
+    for plane in range(2):
+        for hop in (2, 1, 3, 0):
+            target = 2 * lax.rem(chip + hop, 4) + 1 - core
+            if plane == 0:
+                cut_rows(target, facet, offs, turn, wide_re, wide_im, mine)
+            pairs[plane, hop] = to_facet(
+                mine.at[target, plane], pair_buf.at[hop, plane],
+                pair_s.at[plane, hop], pair_r.at[plane, hop], sib,
+            )
+            pairs[plane, hop].start()
+
+    def merge_pair(plane, hop):
+        pairs[plane, hop].wait_recv()
         target = 2 * lax.rem(chip + hop, 4) + core
-        add_blocks(sums.at[hop], [mine.at[target], pair_buf.at[hop]], 0, SUBS)
-
-    merge_pair(2)
-    ring = [
-        to_facet(sums.at[2, low], carry_a, ring_s.at[0], ring_r.at[0], up),
-        to_facet(sums.at[2, high], carry_b, ring_s.at[1], ring_r.at[1], dn),
-        to_facet(sums.at[1, high], from_dn.at[high], ring_s.at[2], ring_r.at[2], up),
-        to_facet(sums.at[3, low], from_up.at[low], ring_s.at[3], ring_r.at[3], dn),
-        to_facet(sums.at[1, low], from_dn.at[low], ring_s.at[4], ring_r.at[4], up),
-        to_facet(sums.at[3, high], from_up.at[high], ring_s.at[5], ring_r.at[5], dn),
+        add_blocks(sums.at[hop, plane], [mine.at[target, plane], pair_buf.at[hop, plane]], 0, SUBS)
+
+    rings = [
+        [
+            to_facet(src, dst, ring_s.at[plane, i], ring_r.at[plane, i], peer)
+            for i, (src, dst, peer) in enumerate((
+                (sums.at[2, plane, low], carry_a.at[plane], up),
+                (sums.at[2, plane, high], carry_b.at[plane], dn),
+                (sums.at[1, plane, high], from_dn.at[plane, high], up),
+                (sums.at[3, plane, low], from_up.at[plane, low], dn),
+                (sums.at[1, plane, low], from_dn.at[plane, low], up),
+                (sums.at[3, plane, high], from_up.at[plane, high], dn),
+            ))
+        ]
+        for plane in range(2)
     ]
-    ring[0].start()
-    ring[1].start()
-    merge_pair(1)
-    ring[2].start()
-    merge_pair(3)
-    ring[3].start()
+
+    def merge_ring(plane):
+        ring = rings[plane]
+        ring[0].wait_recv()
+        add_blocks(sums.at[1, plane, low], [sums.at[1, plane, low], carry_a.at[plane]], 0, 16)
+        ring[4].start()
+        ring[1].wait_recv()
+        add_blocks(sums.at[3, plane, high], [sums.at[3, plane, high], carry_b.at[plane]], 0, 16)
+        ring[5].start()
+
+    def finish(plane):
+        pairs[plane, 0].wait_recv()
+        for step in (3, 4, 2, 5):
+            rings[plane][step].wait_recv()
+        own_target = 2 * chip + core
+        add_blocks(
+            total.at[plane],
+            [mine.at[own_target, plane], pair_buf.at[0, plane], from_dn.at[plane], from_up.at[plane]],
+            0, SUBS,
+        )
+
+    cut_rows(2 * lax.rem(chip + 2, 4) + core, facet, offs, turn, wide_re, wide_im, mine)
+    merge_pair(0, 2)
+    rings[0][0].start()
+    rings[0][1].start()
+    cut_rows(2 * lax.rem(chip + 1, 4) + core, facet, offs, turn, wide_re, wide_im, mine)
+    merge_pair(0, 1)
+    rings[0][2].start()
+    cut_rows(2 * lax.rem(chip + 3, 4) + core, facet, offs, turn, wide_re, wide_im, mine)
+    merge_pair(0, 3)
+    rings[0][3].start()
+    receive_vis, drain_vis = swap(packed, received, 2, vis_r)
+    merge_pair(1, 2)
+    rings[1][0].start()
+    rings[1][1].start()
+    cut_rows(2 * chip + core, facet, offs, turn, wide_re, wide_im, mine)
+    merge_pair(1, 1)
+    merge_pair(1, 3)
     column_phase(facet, offsets, phase)
+    merge_ring(0)
+    rings[1][2].start()
+    rings[1][3].start()
     routing(owners, choice)
-    ring[0].wait_recv()
-    add_blocks(sums.at[1, low], [sums.at[1, low], carry_a], 0, 16)
-    ring[4].start()
-    ring[1].wait_recv()
-    add_blocks(sums.at[3, high], [sums.at[3, high], carry_b], 0, 16)
-    ring[5].start()
-    pairs[0].wait_recv()
-    for step in (2, 3, 4, 5):
-        ring[step].wait_recv()
-    own_target = 2 * chip + core
-    add_blocks(total, [mine.at[own_target], pair_buf.at[0], from_dn, from_up], 0, SUBS)
-
-    receive_rows, drain_rows = swap(total, gathered, 0, first_r)
+    merge_ring(1)
+    finish(0)
+    receive_re, drain_re = swap(total.at[0], gathered.at[0], 0, rows_r.at[0])
+    finish(1)
+    receive_im, drain_im = swap(total.at[1], gathered.at[1], 1, rows_r.at[1])
     keep_load.wait()
     receive_vis()
     vis[...] = mm(choice[...], received[...].reshape(SUBS * SUBS, LANES))
-    receive_rows()
+    receive_re()
+    receive_im()
     columns_to_tiles(gathered, phase, dense, twist, rep, sel, keep, work, folded, tiles)
     visit(tiles, vis, my_tiles)
     tiles_to_columns(my_tiles, phase, dense, twist, rep_t, sel, keep, work, folded_f32, images)
-    receive_images, drain_images = swap(images, out.at[facet], 2, image_r)
-    receive_images()
-
-    def share(index, src, peer):
-        return to_facet(src, src, gath_s.at[index], gath_r.at[index], peer)
-
+
+    swaps = [swap(images.at[plane], out.at[facet, plane], 3 + plane, image_r.at[plane]) for plane in range(2)]
     stores = []
-
-    def store(ref_of):
-        copy = pltpu.make_async_copy(ref_of(out), ref_of(out_hbm), out_sem.at[len(stores)])
+    sends = []
+
+    def store(where):
+        copy = pltpu.make_async_copy(out.at[where], out_hbm.at[where], out_sem.at[len(stores)])
         copy.start()
         stores.append(copy)
 
-    def whole(which):
-        return lambda ref: ref.at[which]
-
-    def part(which, rows):
-        return lambda ref: ref.at[which, rows]
-
-    own = out.at[facet]
-    sends = [share(0, own, up), share(1, own, dn), share(2, own, sib)]
-    for copy in sends:
-        copy.start()
-    store(whole(facet))
-
-    def arrives(index, ref_of):
-        share(index, ref_of(out), sib).wait_recv()
-        store(ref_of)
-
-    def forward(index, ref, peer):
-        sends.append(share(index, ref, peer))
+    def share(plane, index, where, peer):
+        ref = out.at[where]
+        return to_facet(ref, ref, gath_s.at[plane, index], gath_r.at[plane, index], peer)
+
+    def send(plane, index, where, peer):
+        sends.append(share(plane, index, where, peer))
         sends[-1].start()
 
-    share(0, out.at[dn], sib).wait_recv()
-    forward(3, out.at[dn, low], up)
-    forward(5, out.at[dn], sib)
-    store(whole(dn))
-    share(1, out.at[up], sib).wait_recv()
-    forward(4, out.at[up, high], dn)
-    forward(6, out.at[up], sib)
-    store(whole(up))
+    def arrives(plane, index, where):
+        share(plane, index, where, sib).wait_recv()
+
     other = 1 - 2 * core
-    arrives(2, whole(sib))
-    arrives(5, whole(dn + other))
-    arrives(6, whole(up + other))
-    share(3, out.at[opp, low], sib).wait_recv()
-    forward(7, out.at[opp, low], sib)
-    store(part(opp, low))
-    share(4, out.at[opp, high], sib).wait_recv()
-    forward(8, out.at[opp, high], sib)
-    store(part(opp, high))
-    arrives(7, part(opp + other, low))
-    arrives(8, part(opp + other, high))
-    for copy in sends + ring + list(pairs.values()):
+    for plane in range(2):
+        swaps[plane][0]()
+        own = (facet, plane)
+        send(plane, 0, own, up)
+        send(plane, 1, own, dn)
+        send(plane, 2, own, sib)
+        store(own)
+    for plane in range(2):
+        arrives(plane, 0, (dn, plane))
+        send(plane, 3, (dn, plane, low), up)
+        send(plane, 5, (dn, plane), sib)
+        store((dn, plane))
+        arrives(plane, 1, (up, plane))
+        send(plane, 4, (up, plane, high), dn)
+        send(plane, 6, (up, plane), sib)
+        store((up, plane))
+    for plane in range(2):
+        arrives(plane, 2, (sib, plane))
+        store((sib, plane))
+        arrives(plane, 5, (dn + other, plane))
+        store((dn + other, plane))
+        arrives(plane, 6, (up + other, plane))
+        store((up + other, plane))
+    for plane in range(2):
+        arrives(plane, 3, (opp, plane, low))
+        send(plane, 7, (opp, plane, low), sib)
+        store((opp, plane, low))
+        arrives(plane, 4, (opp, plane, high))
+        send(plane, 8, (opp, plane, high), sib)
+        store((opp, plane, high))
+    for plane in range(2):
+        arrives(plane, 7, (opp + other, plane, low))
+        store((opp + other, plane, low))
+        arrives(plane, 8, (opp + other, plane, high))
+        store((opp + other, plane, high))
+    for copy in sends + rings[0] + rings[1] + list(pairs.values()):
         copy.wait_send()
-    for drain in (drain_rows, drain_vis, drain_images):
+    for drain in (drain_re, drain_im, drain_vis, swaps[0][1], swaps[1][1]):
         drain()
     for copy in stores:
         copy.wait()
@@ -649,7 +687,7 @@
 
 
 BIG = 60 * 1024 * 1024
-STRIPS = (FACETS, SUBS, 2, 16, LANES)
+STRIPS = (FACETS, 2, SUBS, 16, LANES)
 WIDE_ROWS = 66 * 128
 
 
@@ -685,8 +723,8 @@
 
 
 def strips_call(shape):
-    block = (SUBS, 2, 16, LANES)
-    half = (16, 2, 16, LANES)
+    block = (2, SUBS, 16, LANES)
+    half = (2, 16, 16, LANES)
     values = (SUBS, VALUES * CAP, LANES)
     vm = pltpu.VMEM
     dma = pltpu.SemaphoreType.DMA
@@ -701,14 +739,14 @@
             vm(TABLE, BF16), vm((512, 512), BF16), vm(STRIPS, BF16),
             vm((4,) + block, BF16), vm((4,) + block, BF16), vm(half, BF16), vm(half, BF16),
             vm(block, BF16), vm(block, BF16), vm(block, BF16), vm(block, BF16),
-            vm(block, F32), vm((512, 256), BF16), vm((512, 256), F32),
+            vm((SUBS, 2, 16, LANES), F32), vm((512, 256), BF16), vm((512, 256), F32),
             vm((512, LANES), BF16), vm((512, LANES), BF16), vm(block, BF16), vm(STRIPS, BF16),
             vm((LANES, LANES), F32), vm((2, SUBS, LANES), F32),
             vm(values, F32), vm(values, BF16), vm(values, BF16),
             vm((VALUES * SUBS, SUBS * SUBS), BF16), vm((VALUES * SUBS, LANES), F32),
-            dma((6,)), dma((10,)),
-            dma((4,)), dma((4,)), dma((6,)), dma((6,)), dma((3, SUBS)),
-            dma((SUBS,)), dma((SUBS,)), dma((SUBS,)), dma((9,)), dma((9,)),
+            dma((6,)), dma((20,)),
+            dma((2, 4)), dma((2, 4)), dma((2, 6)), dma((2, 6)), dma((5, SUBS)),
+            dma((2, SUBS)), dma((SUBS,)), dma((2, SUBS)), dma((2, 9)), dma((2, 9)),
         ],
         compiler_params=pltpu.CompilerParams(
             vmem_limit_bytes=BIG, collective_id=0, has_side_effects=True

time: 69.9 us -> 69.1 us (0.989)
  Pallas kernels: 69.8 us -> 68.9 us
    pallas_call x1, Pallas kernels: 62.6 us -> 61.7 us  [per_device(): strips_call(facet_strips.shape)]
where the time goes in v3:
time: 69.1 us; the launch traced here: 68.9 us
  Pallas kernels  68.9 us (100%)
    pallas_call x1, Pallas kernels, per_device(): strips_call(facet_strips.shape)  61.7 us
    pallas_call x1, Pallas kernels, per_device(): backward_call(facet_strips.shape)  7.11 us

profile of v3, /device:TPU:1, one launch (start us, length us, event | category | flops | bytes accessed | tf_op | source)
XLA Modules:
  0.0 68.9 jit_solution(8245325181017176190)
XLA Ops:
  0.0 61.7 %shard_map.181.strips_hbm = bf16[8,2,32,16,128]{4,3,2,1,0:T(8,128)(2,1)} custom-call(s32[8]{0:T(128)} %offs.3, f32[2,8]{1,0:T(2,128)} %constant.26.clone.turn, f32[32,128]{1,0:T(8,128)} %bitcast.13, f32[1,128]{1,0:T(1,128)} %bitcast.15, bf16[128,128]{1,0:T(8,128)(2,1)} %constant.18.clone.first, s32[1,8]{1,0:T(1,128)} %bitcast.17, s32[1,32]{1,0:T(1,128)} %bitcast.18, ...), custom_call_target="tpu_custom_call" | custom-call | tf_op jit(solution)/shard_map/pallas_call | solution.py:767
  61.8 7.1 %shard_map.182 = bf16[2,4096,128]{2,1,0:T(8,128)(2,1)} custom-call(s32[8]{0:T(128)} %offs.3, f32[2,8]{1,0:T(2,128)} %constant.26.clone.turn, f32[32,128]{1,0:T(8,128)} %bitcast.14, f32[1,128]{1,0:T(1,128)} %bitcast.16, bf16[128,128]{1,0:T(8,128)(2,1)} %constant.18.clone.first, bf16[8,2,32,16,128]{4,3,2,1,0:T(8,128)(2,1)} %shard_map.181.strips_hbm, ...), custom_call_target="tpu_custom_call" | custom-call | tf_op jit(solution)/shard_map/pallas_call | solution.py:773

commit v4 on v3

--- a/solution.py
+++ b/solution.py
@@ -51,14 +51,12 @@
         for r in range(16):
             sel[z, :, r, :, z, r] = 1
     sel = sel.reshape(512, 128)
-    keep = (np.arange(512)[:, None] % 16) == (np.arange(512)[None, :] // 16 % 16)
     return (
         jnp.asarray(dense, BF16),
         jnp.asarray(twist, F32),
         jnp.asarray(rep, BF16),
         jnp.asarray(rep.T, BF16),
         jnp.asarray(sel, BF16),
-        jnp.asarray(keep, BF16),
     )
 
 
@@ -95,7 +93,7 @@
             mid_im[rows, :] = res[RADIX:, u * LANES : (u + 1) * LANES]
         return carry
 
-    lax.fori_loop(0, RADIX // 2, stage_a, 0, unroll=8)
+    lax.fori_loop(0, RADIX // 2, stage_a, 0, unroll=16)
 
     def stage_b(step, carry):
         rows = pl.ds(step * PITCH, RADIX)
@@ -104,7 +102,16 @@
         put(step, res[:RADIX], res[RADIX:])
         return carry
 
-    lax.fori_loop(0, RADIX, stage_b, 0, unroll=16)
+    lax.fori_loop(0, RADIX, stage_b, 0, unroll=32)
+
+
+SMALL = (
+    ((FACETS,), jnp.int32), ((2, FACETS), F32), ((SUBS, LANES), F32), ((1, LANES), F32),
+    ((LANES, LANES), BF16), ((1, FACETS), jnp.int32), ((1, SUBS), jnp.int32),
+    ((LANES, 2, LANES), F32), ((LANES, LANES), F32), ((3, LANES, LANES), jnp.int32), ((1, LANES), jnp.int32),
+    ((SUBS, 2 * LANES), BF16), ((2, SUBS, LANES), F32), ((512, SUBS), BF16), ((SUBS, 512), BF16),
+    ((512, LANES), BF16),
+)
 
 
 def load_strip(strip, row_win, col_win, loads, re, im):
@@ -148,18 +155,21 @@
 
 
 def backward_kernel(
-    offs, turn, row_win, col_win, first, strips_hbm, second_hbm, out_hbm,
-    re, im, mid_re, mid_im, wide_re, wide_im, strips, second, out, second_sem, strip_sem, out_sem,
+    offs_hbm, turn_hbm, row_hbm, col_hbm, first_hbm, strips_hbm, second_hbm, out_hbm,
+    offs, turn, row_win, col_win, first, small_sem, re, im, mid_re, mid_im, wide_re, wide_im, strips, second, out, second_sem, strip_sem, out_sem,
 ):
     def load(which):
         return pltpu.make_async_copy(strips_hbm.at[which], strips.at[which], strip_sem.at[which])
 
+    pairs = zip((offs_hbm, turn_hbm, row_hbm, col_hbm, first_hbm), (offs, turn, row_win, col_win, first))
+    small = [pltpu.make_async_copy(src, dst, small_sem.at[i]) for i, (src, dst) in enumerate(pairs)]
+    for copy in small:
+        copy.start()
     for which in range(FACETS):
         load(which).start()
     table = pltpu.make_async_copy(second_hbm, second, second_sem)
     table.start()
     facet = lax.axis_index("facet")
-    row_win = row_win[...].T
 
     def clear(step, carry):
         rows = pl.ds(pl.multiple_of(step * 128, 128), 128)
@@ -168,6 +178,8 @@
         return carry
 
     lax.fori_loop(0, WIDE_ROWS // 128, clear, 0, unroll=2)
+    for copy in small:
+        copy.wait()
 
     def place(which, carry):
         load(which).wait()
@@ -197,7 +209,7 @@
         im[rows, :] = imag
 
     transform_rows(fetch, mid_re, mid_im, first, second, put)
-    scale = col_win[...]
+    row_win, scale = row_win[...].T, col_win[...]
     quarter = LONG // 4
     copies = []
     for block in range(RADIX):
@@ -415,6 +427,12 @@
     phase[1] = sine
 
 
+def same_pixel(keep):
+    for part in range(4):
+        rows = slice(part * 128, part * 128 + 128)
+        keep[rows, :] = as_bf(iota((128, 512), 0) % TS == iota((128, 512), 1) // TS % TS)
+
+
 def routing(owners, choice):
     square = (SUBS, SUBS)
     up, across = iota(square, 0), iota(square, 1)
@@ -447,9 +465,17 @@
 
 
 def facet_to_strips_kernel(
+    strip_hbm, second_hbm, *rest
+):
+    count = len(SMALL)
+    small_hbm, out_hbm, small = rest[:count], rest[count], rest[count + 1 : 2 * count + 1]
+    strips_body(strip_hbm, second_hbm, small_hbm, out_hbm, small, *small, *rest[2 * count + 1 :])
+
+
+def strips_body(
+    strip_hbm, second_hbm, small_hbm, out_hbm, small,
     offs, turn, row_win, col_win, first, offsets, owners, measured, weight, pixels, counts,
-    dense, twist, rep, rep_t, sel, strip_hbm, second_hbm, keep_hbm,
-    out_hbm,
+    dense, twist, rep, rep_t, sel,
     strip, re, im, mid_re, mid_im, wide_re, wide_im, second, keep, mine,
     pair_buf, sums, carry_a, carry_b, from_dn, from_up, total, gathered,
     work, folded, folded_f32, tiles, my_tiles, images, out,
@@ -482,9 +508,13 @@
         for i in range(4)
     ]
     second_load = pltpu.make_async_copy(second_hbm, second, load_sem.at[4])
-    keep_load = pltpu.make_async_copy(keep_hbm, keep, load_sem.at[5])
-    for copy in loads + [second_load, keep_load]:
+    small_loads = [
+        pltpu.make_async_copy(src, dst, load_sem.at[5 + i]) for i, (src, dst) in enumerate(zip(small_hbm, small))
+    ]
+    for copy in loads + small_loads + [second_load]:
         copy.start()
+    for copy in small_loads:
+        copy.wait()
     masked_weights(weight, counts, masked)
     pack_visibilities(measured, masked, pixels, staged, packed)
     load_strip(strip, row_win, col_win, loads, re, im)
@@ -497,6 +527,14 @@
             src_ref=src, dst_ref=dst, send_sem=ssem, recv_sem=rsem,
             device_id={"facet": peer}, device_id_type=MESH,
         )
+
+    x_at = [lax.rem(me // 8 + i, 4) * 8 for i in range(4)]
+    z_at = [lax.rem(lax.rem(me, 8) + i, 8) for i in range(8)]
+    steps = sorted(
+        ((i, j) for i in range(4) for j in range(8) if i + j),
+        key=lambda ij: -(min(ij[0], 4 - ij[0]) + min(ij[1], 8 - ij[1])),
+    )
+    peers = [x_at[i] + z_at[j] for i, j in steps]
 
     def swap(src_of, dst, kind, rsem):
         def copy_to(peer, slot):
@@ -506,10 +544,6 @@
                 device_id={"sub": peer}, device_id_type=MESH,
             )
 
-        def send(step, carry):
-            copy_to(lax.rem(me + step, SUBS), me).start()
-            return carry
-
         def receive(step, carry):
             peer = lax.rem(me + SUBS - step, SUBS)
             copy_to(peer, peer).wait_recv()
@@ -519,7 +553,8 @@
             copy_to(lax.rem(me + step, SUBS), me).wait_send()
             return carry
 
-        lax.fori_loop(1, SUBS, send, 0)
+        for peer in peers:
+            copy_to(peer, me).start()
         dst[me] = src_of[me]
         return (
             lambda: lax.fori_loop(1, SUBS, receive, 0),
@@ -600,12 +635,12 @@
     rings[1][2].start()
     rings[1][3].start()
     routing(owners, choice)
+    same_pixel(keep)
     merge_ring(1)
     finish(0)
     receive_re, drain_re = swap(total.at[0], gathered.at[0], 0, rows_r.at[0])
     finish(1)
     receive_im, drain_im = swap(total.at[1], gathered.at[1], 1, rows_r.at[1])
-    keep_load.wait()
     receive_vis()
     vis[...] = mm(choice[...], received[...].reshape(SUBS * SUBS, LANES))
     receive_re()
@@ -615,6 +650,10 @@
     tiles_to_columns(my_tiles, phase, dense, twist, rep_t, sel, keep, work, folded_f32, images)
 
     swaps = [swap(images.at[plane], out.at[facet, plane], 3 + plane, image_r.at[plane]) for plane in range(2)]
+    for copy in rings[0] + rings[1] + list(pairs.values()):
+        copy.wait_send()
+    for drain in (drain_vis, drain_re, drain_im):
+        drain()
     stores = []
     sends = []
 
@@ -642,6 +681,8 @@
         send(plane, 1, own, dn)
         send(plane, 2, own, sib)
         store(own)
+    for plane in range(2):
+        swaps[plane][1]()
     for plane in range(2):
         arrives(plane, 0, (dn, plane))
         send(plane, 3, (dn, plane, low), up)
@@ -670,10 +711,8 @@
         store((opp + other, plane, low))
         arrives(plane, 8, (opp + other, plane, high))
         store((opp + other, plane, high))
-    for copy in sends + rings[0] + rings[1] + list(pairs.values()):
+    for copy in sends:
         copy.wait_send()
-    for drain in (drain_re, drain_im, drain_vis, swaps[0][1], swaps[1][1]):
-        drain()
     for copy in stores:
         copy.wait()
 
@@ -707,9 +746,11 @@
     return pl.pallas_call(
         backward_kernel,
         out_shape=jax.ShapeDtypeStruct(shape, BF16),
-        in_specs=smem_specs(2) + vmem_specs(3) + any_specs(2),
+        in_specs=any_specs(7),
         out_specs=pl.BlockSpec(memory_space=pl.ANY),
-        scratch_shapes=row_scratch()
+        scratch_shapes=[(pltpu.SMEM if i < 2 else pltpu.VMEM)(*item) for i, item in enumerate(SMALL[:5])]
+        + [pltpu.SemaphoreType.DMA((5,))]
+        + row_scratch()
         + [
             pltpu.VMEM(STRIPS, BF16),
             pltpu.VMEM(TABLE, BF16),
@@ -731,9 +772,10 @@
     return pl.pallas_call(
         facet_to_strips_kernel,
         out_shape=jax.ShapeDtypeStruct(STRIPS, BF16),
-        in_specs=smem_specs(2) + vmem_specs(14) + any_specs(3),
+        in_specs=any_specs(2 + len(SMALL)),
         out_specs=pl.BlockSpec(memory_space=pl.ANY),
-        scratch_shapes=[vm(shape, BF16)]
+        scratch_shapes=[(pltpu.SMEM if i < 2 else vm)(*item) for i, item in enumerate(SMALL)]
+        + [vm(shape, BF16)]
         + row_scratch()
         + [
             vm(TABLE, BF16), vm((512, 512), BF16), vm(STRIPS, BF16),
@@ -744,7 +786,7 @@
             vm((LANES, LANES), F32), vm((2, SUBS, LANES), F32),
             vm(values, F32), vm(values, BF16), vm(values, BF16),
             vm((VALUES * SUBS, SUBS * SUBS), BF16), vm((VALUES * SUBS, LANES), F32),
-            dma((6,)), dma((20,)),
+            dma((5 + len(SMALL),)), dma((20,)),
             dma((2, 4)), dma((2, 4)), dma((2, 6)), dma((2, 6)), dma((5, SUBS)),
             dma((2, SUBS)), dma((SUBS,)), dma((2, SUBS)), dma((2, 9)), dma((2, 9)),
         ],
@@ -759,16 +801,16 @@
     tile_owner, measured, vis_weight, uvw_pixels, vis_count,
 ):
     first, second = row_tables()
-    dense, twist, rep, rep_t, sel, keep = col_tables()
+    dense, twist, rep, rep_t, sel = col_tables()
     eighth = 2 * np.pi * np.arange(FACETS) / FACETS
     turn = jnp.asarray(np.stack([np.cos(eighth), np.sin(eighth)]), F32)
     row_win = row_window.reshape(LONG // LANES, LANES)
     col_win = col_window.reshape(1, LANES)
     strips = strips_call(facet_strips.shape)(
-        row_offsets, turn, row_win, col_win, first,
+        facet_strips, second, row_offsets, turn, row_win, col_win, first,
         col_offsets.reshape(1, FACETS), tile_owner.reshape(1, SUBS), measured[0, 0],
         vis_weight[0, 0], jnp.transpose(uvw_pixels[0, 0], (1, 0, 2)), vis_count.reshape(1, LANES),
-        dense, twist, rep, rep_t, sel, facet_strips, second, keep,
+        dense, twist, rep, rep_t, sel,
     )
     return backward_call(facet_strips.shape)(
         row_offsets, turn, row_win, col_win, first, strips, second

time: 69.1 us -> 64.1 us (0.928)
  Pallas kernels: 68.9 us -> 64 us
    pallas_call x1, Pallas kernels: 61.7 us -> 58.1 us  [per_device(): strips_call(facet_strips.shape)]
    pallas_call x1, Pallas kernels: 7.11 us -> 5.84 us  [per_device(): backward_call(facet_strips.shape)]
where the time goes in v4:
time: 64.1 us; the launch traced here: 64 us
  Pallas kernels  64 us (100%)
    pallas_call x1, Pallas kernels, per_device(): strips_call(facet_strips.shape)  58.1 us
    pallas_call x1, Pallas kernels, per_device(): backward_call(facet_strips.shape)  5.84 us

profile of v4, /device:TPU:1, one launch (start us, length us, event | category | flops | bytes accessed | tf_op | source)
XLA Modules:
  0.0 64.0 jit_solution(2774128365444431769)
XLA Ops:
  0.0 58.1 %shard_map.172.strips_hbm = bf16[8,2,32,16,128]{4,3,2,1,0:T(8,128)(2,1)} custom-call(bf16[2,4096,128]{2,1,0:T(8,128)(2,1)} %strip_hbm.1, bf16[64,128,128]{2,1,0:T(8,128)(2,1)} %constant.17.clone.second_hbm, s32[8]{0:T(128)} %offs_hbm.1, f32[2,8]{1,0:T(2,128)} %constant.23.clone.rest_1_.turn_hbm, f32[32,128]{1,0:T(8,128)} %bitcast.13, f32[1,128]{1,0:T(1,128)} %bitcast.15, ...), custom_call_target="tpu_custom_call" | custom-call | tf_op jit(solution)/shard_map/pallas_call | solution.py:809
  58.1 5.8 %shard_map.173 = bf16[2,4096,128]{2,1,0:T(8,128)(2,1)} custom-call(s32[8]{0:T(128)} %offs_hbm.1, f32[2,8]{1,0:T(2,128)} %constant.23.clone.rest_1_.turn_hbm, f32[32,128]{1,0:T(8,128)} %bitcast.14, f32[1,128]{1,0:T(1,128)} %bitcast.16, bf16[128,128]{1,0:T(8,128)(2,1)} %constant.16.clone.rest_4_.first_hbm, bf16[8,2,32,16,128]{4,3,2,1,0:T(8,128)(2,1)} %shard_map.172.strips_hbm, ...), custom_call_target="tpu_custom_call" | custom-call | tf_op jit(solution)/shard_map/pallas_call | solution.py:815

commit v5 on v4

--- a/solution.py
+++ b/solution.py
@@ -72,6 +72,24 @@
     return lax.dot_general(first, other, (((0,), (0,)), ((), ())), preferred_element_type=F32)
 
 
+STEPS = sorted(
+    ((i, j) for i in range(4) for j in range(8)),
+    key=lambda ij: -(min(ij[0], 4 - ij[0]) + min(ij[1], 8 - ij[1])),
+)
+SEEN_FROM = [STEPS.index(((4 - i) % 4, (8 - j) % 8)) for i, j in STEPS]
+
+
+def devices_by_distance(me):
+    x, z = lax.div(me, 8), lax.rem(me, 8)
+    x_at = [lax.rem(x + i, 4) * 8 for i in range(4)]
+    z_at = [lax.rem(z + i, 8) for i in range(8)]
+    return [x_at[i] + z_at[j] for i, j in STEPS]
+
+
+def wide_rows(peers):
+    return [lax.div(peer, 4) * WIDE + lax.rem(peer, 4) * 16 for peer in peers]
+
+
 PITCH = RADIX + 1
 WIDE = 2 * RADIX + 1
 
@@ -141,17 +159,16 @@
     transform_rows(fetch, mid_re, mid_im, first, second, put)
 
 
-def cut_rows(which, facet, offs, turn, wide_re, wide_im, out):
+def cut_rows(which, facet, offs, turn, places, wide_re, wide_im, out):
     base = offs[which]
     index = (facet * base) & (FACETS - 1)
     cosine, sine = turn[0, index], turn[1, index]
     start = WIDE + base // RADIX * WIDE + base % RADIX
-    for part in range(8):
-        rows = pl.ds(start + part * WIDE, RADIX)
+    for i, place in enumerate(places):
+        rows = pl.ds(start + place, 16)
         real, imag = wide_re[rows, :], wide_im[rows, :]
-        blocks = pl.ds(part * 4, 4)
-        out[which, 0, blocks] = (cosine * real + sine * imag).astype(BF16).reshape(4, 16, LANES)
-        out[which, 1, blocks] = (cosine * imag - sine * real).astype(BF16).reshape(4, 16, LANES)
+        out[which, i // 16, 0, i % 16] = (cosine * real + sine * imag).astype(BF16)
+        out[which, i // 16, 1, i % 16] = (cosine * imag - sine * real).astype(BF16)
 
 
 def backward_kernel(
@@ -181,17 +198,18 @@
     for copy in small:
         copy.wait()
 
+    places = wide_rows(devices_by_distance(lax.axis_index("sub")))
+
     def place(which, carry):
         load(which).wait()
         base = offs[which]
         index = (facet * base) & (FACETS - 1)
         cosine, sine = turn[0, index], turn[1, index]
         start = WIDE + base // RADIX * WIDE + base % RADIX
-        for part in range(8):
-            rows = pl.ds(start + part * WIDE, RADIX)
-            blocks = pl.ds(part * 4, 4)
-            real = strips[which, 0, blocks].reshape(RADIX, LANES).astype(F32)
-            imag = strips[which, 1, blocks].reshape(RADIX, LANES).astype(F32)
+        for i, place_at in enumerate(places):
+            rows = pl.ds(start + place_at, 16)
+            real = strips[which, i // 16, 0, i % 16].astype(F32)
+            imag = strips[which, i // 16, 1, i % 16].astype(F32)
             wide_re[rows, :] = wide_re[rows, :] + (cosine * real - sine * imag)
             wide_im[rows, :] = wide_im[rows, :] - (sine * real + cosine * imag)
         return carry
@@ -489,7 +507,8 @@
     sib = facet + 1 - 2 * core
     up, dn = lax.rem(facet + 2, FACETS), lax.rem(facet + 6, FACETS)
     opp = lax.rem(facet + 4, FACETS)
-    low, high = pl.ds(0, 16), pl.ds(16, 16)
+    peers = devices_by_distance(me)
+    places = wide_rows(peers)
 
     barrier = pltpu.get_barrier_semaphore()
 
@@ -511,7 +530,7 @@
     small_loads = [
         pltpu.make_async_copy(src, dst, load_sem.at[5 + i]) for i, (src, dst) in enumerate(zip(small_hbm, small))
     ]
-    for copy in loads + small_loads + [second_load]:
+    for copy in small_loads + loads + [second_load]:
         copy.start()
     for copy in small_loads:
         copy.wait()
@@ -528,106 +547,125 @@
             device_id={"facet": peer}, device_id_type=MESH,
         )
 
-    x_at = [lax.rem(me // 8 + i, 4) * 8 for i in range(4)]
-    z_at = [lax.rem(lax.rem(me, 8) + i, 8) for i in range(8)]
-    steps = sorted(
-        ((i, j) for i in range(4) for j in range(8) if i + j),
-        key=lambda ij: -(min(ij[0], 4 - ij[0]) + min(ij[1], 8 - ij[1])),
-    )
-    peers = [x_at[i] + z_at[j] for i, j in steps]
-
-    def swap(src_of, dst, kind, rsem):
-        def copy_to(peer, slot):
-            return pltpu.make_async_remote_copy(
-                src_ref=src_of.at[peer], dst_ref=dst.at[slot],
-                send_sem=send_s.at[kind, peer], recv_sem=rsem.at[slot],
-                device_id={"sub": peer}, device_id_type=MESH,
-            )
-
-        def receive(step, carry):
-            peer = lax.rem(me + SUBS - step, SUBS)
-            copy_to(peer, peer).wait_recv()
+    def to_sub(src, dst, ssem, rsem, peer):
+        return pltpu.make_async_remote_copy(
+            src_ref=src, dst_ref=dst, send_sem=ssem, recv_sem=rsem,
+            device_id={"sub": peer}, device_id_type=MESH,
+        )
+
+    def others(body):
+        def one(step, carry):
+            body(lax.rem(me + step, SUBS))
             return carry
 
-        def drain(step, carry):
-            copy_to(lax.rem(me + step, SUBS), me).wait_send()
-            return carry
-
-        for peer in peers:
-            copy_to(peer, me).start()
-        dst[me] = src_of[me]
-        return (
-            lambda: lax.fori_loop(1, SUBS, receive, 0),
-            lambda: lax.fori_loop(1, SUBS, drain, 0),
+        lax.fori_loop(1, SUBS, one, 0)
+
+    def vis_copy(peer, slot, sem):
+        return to_sub(packed.at[peer], received.at[slot], send_s.at[0, sem], vis_r.at[slot], peer)
+
+    def send_vis():
+        for i, peer in enumerate(peers[:-1]):
+            vis_copy(peer, me, i).start()
+        received[me] = packed[me]
+
+    def rows_copy(half, block, peer, slot):
+        return to_sub(
+            total.at[half, :, block], gathered.at[:, slot], send_s.at[1, half * 16 + block], rows_r.at[slot], peer
         )
 
+    def send_rows(half):
+        for block in range(16 - half):
+            rows_copy(half, block, peers[half * 16 + block], me).start()
+
+    def image_copy(i, peer):
+        spot = SEEN_FROM[i]
+        return to_sub(
+            images.at[:, peer], out.at[facet, spot // 16, :, spot % 16], send_s.at[2, i], image_r.at[spot], peer
+        )
+
+    def image_arrives(spot):
+        to_sub(
+            images.at[:, 0], out.at[facet, lax.div(spot, 16), :, lax.rem(spot, 16)],
+            send_s.at[2, 0], image_r.at[spot], peers[0],
+        ).wait_recv()
+
+    def cut(which):
+        cut_rows(which, facet, offs, turn, places, wide_re, wide_im, mine)
+
     pairs = {}
-    for plane in range(2):
+    for half in range(2):
         for hop in (2, 1, 3, 0):
             target = 2 * lax.rem(chip + hop, 4) + 1 - core
-            if plane == 0:
-                cut_rows(target, facet, offs, turn, wide_re, wide_im, mine)
-            pairs[plane, hop] = to_facet(
-                mine.at[target, plane], pair_buf.at[hop, plane],
-                pair_s.at[plane, hop], pair_r.at[plane, hop], sib,
+            if half == 0:
+                cut(target)
+            pairs[half, hop] = to_facet(
+                mine.at[target, half], pair_buf.at[hop, half],
+                pair_s.at[half, hop], pair_r.at[half, hop], sib,
             )
-            pairs[plane, hop].start()
-
-    def merge_pair(plane, hop):
-        pairs[plane, hop].wait_recv()
+            pairs[half, hop].start()
+
+    def merge_pair(half, hop):
+        pairs[half, hop].wait_recv()
         target = 2 * lax.rem(chip + hop, 4) + core
-        add_blocks(sums.at[hop, plane], [mine.at[target, plane], pair_buf.at[hop, plane]], 0, SUBS)
+        for plane in range(2):
+            add_blocks(
+                sums.at[hop, half, plane], [mine.at[target, half, plane], pair_buf.at[hop, half, plane]], 0, 16
+            )
 
     rings = [
         [
-            to_facet(src, dst, ring_s.at[plane, i], ring_r.at[plane, i], peer)
+            to_facet(src, dst, ring_s.at[half, i], ring_r.at[half, i], peer)
             for i, (src, dst, peer) in enumerate((
-                (sums.at[2, plane, low], carry_a.at[plane], up),
-                (sums.at[2, plane, high], carry_b.at[plane], dn),
-                (sums.at[1, plane, high], from_dn.at[plane, high], up),
-                (sums.at[3, plane, low], from_up.at[plane, low], dn),
-                (sums.at[1, plane, low], from_dn.at[plane, low], up),
-                (sums.at[3, plane, high], from_up.at[plane, high], dn),
+                (sums.at[2, half, 0], carry_a.at[half], up),
+                (sums.at[2, half, 1], carry_b.at[half], dn),
+                (sums.at[1, half, 1], from_dn.at[half, 1], up),
+                (sums.at[3, half, 0], from_up.at[half, 0], dn),
+                (sums.at[1, half, 0], from_dn.at[half, 0], up),
+                (sums.at[3, half, 1], from_up.at[half, 1], dn),
             ))
         ]
-        for plane in range(2)
+        for half in range(2)
     ]
 
-    def merge_ring(plane):
-        ring = rings[plane]
+    def merge_ring(half):
+        ring = rings[half]
         ring[0].wait_recv()
-        add_blocks(sums.at[1, plane, low], [sums.at[1, plane, low], carry_a.at[plane]], 0, 16)
+        add_blocks(sums.at[1, half, 0], [sums.at[1, half, 0], carry_a.at[half]], 0, 16)
         ring[4].start()
         ring[1].wait_recv()
-        add_blocks(sums.at[3, plane, high], [sums.at[3, plane, high], carry_b.at[plane]], 0, 16)
+        add_blocks(sums.at[3, half, 1], [sums.at[3, half, 1], carry_b.at[half]], 0, 16)
         ring[5].start()
 
-    def finish(plane):
-        pairs[plane, 0].wait_recv()
-        for step in (3, 4, 2, 5):
-            rings[plane][step].wait_recv()
+    def finish(half):
+        pairs[half, 0].wait_recv()
         own_target = 2 * chip + core
-        add_blocks(
-            total.at[plane],
-            [mine.at[own_target, plane], pair_buf.at[0, plane], from_dn.at[plane], from_up.at[plane]],
-            0, SUBS,
-        )
-
-    cut_rows(2 * lax.rem(chip + 2, 4) + core, facet, offs, turn, wide_re, wide_im, mine)
+        for plane, steps in ((0, (3, 4)), (1, (2, 5))):
+            for step in steps:
+                rings[half][step].wait_recv()
+            add_blocks(
+                total.at[half, plane],
+                [
+                    ref.at[half, plane]
+                    for ref in (mine.at[own_target], pair_buf.at[0], from_dn, from_up)
+                ],
+                0, 16,
+            )
+
+    cut(2 * lax.rem(chip + 2, 4) + core)
     merge_pair(0, 2)
     rings[0][0].start()
     rings[0][1].start()
-    cut_rows(2 * lax.rem(chip + 1, 4) + core, facet, offs, turn, wide_re, wide_im, mine)
+    cut(2 * lax.rem(chip + 1, 4) + core)
     merge_pair(0, 1)
     rings[0][2].start()
-    cut_rows(2 * lax.rem(chip + 3, 4) + core, facet, offs, turn, wide_re, wide_im, mine)
+    cut(2 * lax.rem(chip + 3, 4) + core)
     merge_pair(0, 3)
     rings[0][3].start()
-    receive_vis, drain_vis = swap(packed, received, 2, vis_r)
+    send_vis()
     merge_pair(1, 2)
     rings[1][0].start()
     rings[1][1].start()
-    cut_rows(2 * chip + core, facet, offs, turn, wide_re, wide_im, mine)
+    cut(2 * chip + core)
     merge_pair(1, 1)
     merge_pair(1, 3)
     column_phase(facet, offsets, phase)
@@ -638,22 +676,34 @@
     same_pixel(keep)
     merge_ring(1)
     finish(0)
-    receive_re, drain_re = swap(total.at[0], gathered.at[0], 0, rows_r.at[0])
+    send_rows(0)
     finish(1)
-    receive_im, drain_im = swap(total.at[1], gathered.at[1], 1, rows_r.at[1])
-    receive_vis()
+    send_rows(1)
+    for plane in range(2):
+        gathered[plane, me] = total[1, plane, 15]
+    others(lambda peer: vis_copy(peer, peer, 0).wait_recv())
     vis[...] = mm(choice[...], received[...].reshape(SUBS * SUBS, LANES))
-    receive_re()
-    receive_im()
+    others(lambda peer: rows_copy(0, 0, peer, peer).wait_recv())
     columns_to_tiles(gathered, phase, dense, twist, rep, sel, keep, work, folded, tiles)
     visit(tiles, vis, my_tiles)
     tiles_to_columns(my_tiles, phase, dense, twist, rep_t, sel, keep, work, folded_f32, images)
 
-    swaps = [swap(images.at[plane], out.at[facet, plane], 3 + plane, image_r.at[plane]) for plane in range(2)]
+    for i, peer in enumerate(peers[:-1]):
+        image_copy(i, peer).start()
+    for plane in range(2):
+        out[facet, 1, plane, 15] = images[plane, me]
     for copy in rings[0] + rings[1] + list(pairs.values()):
         copy.wait_send()
-    for drain in (drain_vis, drain_re, drain_im):
-        drain()
+
+    def drain(kind, src):
+        def one(step, carry):
+            to_sub(src, src, send_s.at[kind, step], vis_r.at[0], sib).wait_send()
+            return carry
+
+        lax.fori_loop(0, SUBS - 1, one, 0)
+
+    drain(0, packed.at[0])
+    drain(1, total.at[0, :, 0])
     stores = []
     sends = []
 
@@ -662,55 +712,67 @@
         copy.start()
         stores.append(copy)
 
-    def share(plane, index, where, peer):
+    def share(half, index, where, peer):
         ref = out.at[where]
-        return to_facet(ref, ref, gath_s.at[plane, index], gath_r.at[plane, index], peer)
-
-    def send(plane, index, where, peer):
-        sends.append(share(plane, index, where, peer))
+        return to_facet(ref, ref, gath_s.at[half, index], gath_r.at[half, index], peer)
+
+    def send(half, index, where, peer):
+        sends.append(share(half, index, where, peer))
         sends[-1].start()
 
-    def arrives(plane, index, where):
-        share(plane, index, where, sib).wait_recv()
+    def arrives(half, index, where):
+        share(half, index, where, sib).wait_recv()
+
+    def one_image(spot, carry):
+        image_arrives(spot)
+        return carry
+
+    def own_half(half):
+        lax.fori_loop(16 * half, 16 + 15 * half, one_image, 0)
+        own = (facet, half)
+        send(half, 0, own, up)
+        send(half, 1, own, dn)
+        send(half, 2, own, sib)
+        store(own)
+
+    def onward(half):
+        arrives(half, 0, (dn, half))
+        send(half, 3, (dn, half, 0), up)
+        send(half, 5, (dn, half), sib)
+        store((dn, half))
+        arrives(half, 1, (up, half))
+        send(half, 4, (up, half, 1), dn)
+        send(half, 6, (up, half), sib)
+        store((up, half))
+
+    def opposite(half):
+        arrives(half, 3, (opp, half, 0))
+        send(half, 7, (opp, half, 0), sib)
+        store((opp, half, 0))
+        arrives(half, 4, (opp, half, 1))
+        send(half, 8, (opp, half, 1), sib)
+        store((opp, half, 1))
 
     other = 1 - 2 * core
-    for plane in range(2):
-        swaps[plane][0]()
-        own = (facet, plane)
-        send(plane, 0, own, up)
-        send(plane, 1, own, dn)
-        send(plane, 2, own, sib)
-        store(own)
-    for plane in range(2):
-        swaps[plane][1]()
-    for plane in range(2):
-        arrives(plane, 0, (dn, plane))
-        send(plane, 3, (dn, plane, low), up)
-        send(plane, 5, (dn, plane), sib)
-        store((dn, plane))
-        arrives(plane, 1, (up, plane))
-        send(plane, 4, (up, plane, high), dn)
-        send(plane, 6, (up, plane), sib)
-        store((up, plane))
-    for plane in range(2):
-        arrives(plane, 2, (sib, plane))
-        store((sib, plane))
-        arrives(plane, 5, (dn + other, plane))
-        store((dn + other, plane))
-        arrives(plane, 6, (up + other, plane))
-        store((up + other, plane))
-    for plane in range(2):
-        arrives(plane, 3, (opp, plane, low))
-        send(plane, 7, (opp, plane, low), sib)
-        store((opp, plane, low))
-        arrives(plane, 4, (opp, plane, high))
-        send(plane, 8, (opp, plane, high), sib)
-        store((opp, plane, high))
-    for plane in range(2):
-        arrives(plane, 7, (opp + other, plane, low))
-        store((opp + other, plane, low))
-        arrives(plane, 8, (opp + other, plane, high))
-        store((opp + other, plane, high))
+    own_half(1)
+    own_half(0)
+    drain(2, images.at[:, 0])
+    onward(1)
+    onward(0)
+    opposite(1)
+    for half in (1, 0):
+        arrives(half, 2, (sib, half))
+        store((sib, half))
+        arrives(half, 5, (dn + other, half))
+        store((dn + other, half))
+        arrives(half, 6, (up + other, half))
+        store((up + other, half))
+    opposite(0)
+    for half in (1, 0):
+        arrives(half, 7, (opp + other, half, 0))
+        store((opp + other, half, 0))
+        arrives(half, 8, (opp + other, half, 1))
+        store((opp + other, half, 1))
     for copy in sends:
         copy.wait_send()
     for copy in stores:
@@ -726,7 +788,7 @@
 
 
 BIG = 60 * 1024 * 1024
-STRIPS = (FACETS, 2, SUBS, 16, LANES)
+STRIPS = (FACETS, 2, 2, 16, 16, LANES)
 WIDE_ROWS = 66 * 128
 
 
@@ -765,6 +827,7 @@
 
 def strips_call(shape):
     block = (2, SUBS, 16, LANES)
+    halves = (2, 2, 16, 16, LANES)
     half = (2, 16, 16, LANES)
     values = (SUBS, VALUES * CAP, LANES)
     vm = pltpu.VMEM
@@ -779,16 +842,16 @@
         + row_scratch()
         + [
             vm(TABLE, BF16), vm((512, 512), BF16), vm(STRIPS, BF16),
-            vm((4,) + block, BF16), vm((4,) + block, BF16), vm(half, BF16), vm(half, BF16),
-            vm(block, BF16), vm(block, BF16), vm(block, BF16), vm(block, BF16),
+            vm((4,) + halves, BF16), vm((4,) + halves, BF16), vm(half, BF16), vm(half, BF16),
+            vm(halves, BF16), vm(halves, BF16), vm(halves, BF16), vm(block, BF16),
             vm((SUBS, 2, 16, LANES), F32), vm((512, 256), BF16), vm((512, 256), F32),
             vm((512, LANES), BF16), vm((512, LANES), BF16), vm(block, BF16), vm(STRIPS, BF16),
             vm((LANES, LANES), F32), vm((2, SUBS, LANES), F32),
             vm(values, F32), vm(values, BF16), vm(values, BF16),
             vm((VALUES * SUBS, SUBS * SUBS), BF16), vm((VALUES * SUBS, LANES), F32),
             dma((5 + len(SMALL),)), dma((20,)),
-            dma((2, 4)), dma((2, 4)), dma((2, 6)), dma((2, 6)), dma((5, SUBS)),
-            dma((2, SUBS)), dma((SUBS,)), dma((2, SUBS)), dma((2, 9)), dma((2, 9)),
+            dma((2, 4)), dma((2, 4)), dma((2, 6)), dma((2, 6)), dma((3, SUBS)),
+            dma((SUBS,)), dma((SUBS,)), dma((SUBS,)), dma((2, 9)), dma((2, 9)),
         ],
         compiler_params=pltpu.CompilerParams(
             vmem_limit_bytes=BIG, collective_id=0, has_side_effects=True

time: 64.1 us -> 65.3 us (1.019)
  Pallas kernels: 64 us -> 65.3 us
    pallas_call x1, Pallas kernels: 58.1 us -> 59.1 us  [per_device(): strips_call(facet_strips.shape)]
where the time goes in v5:
time: 65.3 us
  Pallas kernels  65.3 us (100%)
    pallas_call x1, Pallas kernels, per_device(): strips_call(facet_strips.shape)  59.1 us
    pallas_call x1, Pallas kernels, per_device(): backward_call(facet_strips.shape)  6.12 us

profile of v5, /device:TPU:1, one launch (start us, length us, event | category | flops | bytes accessed | tf_op | source)
XLA Modules:
  0.0 65.3 jit_solution(7346765921939318895)
XLA Ops:
  0.0 59.1 %shard_map.172.strips_hbm = bf16[8,2,2,16,16,128]{5,4,3,2,1,0:T(8,128)(2,1)} custom-call(bf16[2,4096,128]{2,1,0:T(8,128)(2,1)} %strip_hbm.1, bf16[64,128,128]{2,1,0:T(8,128)(2,1)} %constant.17.clone.second_hbm, s32[8]{0:T(128)} %offs_hbm.1, f32[2,8]{1,0:T(2,128)} %constant.23.clone.rest_1_.turn_hbm, f32[32,128]{1,0:T(8,128)} %bitcast.13, f32[1,128]{1,0:T(1,128)} %bitcast.15, ...), custom_call_target="tpu_custom_call" | custom-call | tf_op jit(solution)/shard_map/pallas_call | solution.py:872
  59.2 6.1 %shard_map.173 = bf16[2,4096,128]{2,1,0:T(8,128)(2,1)} custom-call(s32[8]{0:T(128)} %offs_hbm.1, f32[2,8]{1,0:T(2,128)} %constant.23.clone.rest_1_.turn_hbm, f32[32,128]{1,0:T(8,128)} %bitcast.14, f32[1,128]{1,0:T(1,128)} %bitcast.16, bf16[128,128]{1,0:T(8,128)(2,1)} %constant.16.clone.rest_4_.first_hbm, ...), custom_call_target="tpu_custom_call" | custom-call | tf_op jit(solution)/shard_map/pallas_call | solution.py:878

commit v6 on v5

--- a/solution.py
+++ b/solution.py
@@ -688,8 +688,8 @@
     visit(tiles, vis, my_tiles)
     tiles_to_columns(my_tiles, phase, dense, twist, rep_t, sel, keep, work, folded_f32, images)
 
-    for i, peer in enumerate(peers[:-1]):
-        image_copy(i, peer).start()
+    for i in reversed(range(SUBS - 1)):
+        image_copy(i, peers[i]).start()
     for plane in range(2):
         out[facet, 1, plane, 15] = images[plane, me]
     for copy in rings[0] + rings[1] + list(pairs.values()):

time: 65.3 us -> 63.2 us (0.968)
  Pallas kernels: 65.3 us -> 63.1 us
    pallas_call x1, Pallas kernels: 59.1 us -> 57 us  [per_device(): strips_call(facet_strips.shape)]
where the time goes in v6:
time: 63.2 us; the launch traced here: 63.1 us
  Pallas kernels  63.1 us (100%)
    pallas_call x1, Pallas kernels, per_device(): strips_call(facet_strips.shape)  57 us
    pallas_call x1, Pallas kernels, per_device(): backward_call(facet_strips.shape)  6.12 us

profile of v6, /device:TPU:1, one launch (start us, length us, event | category | flops | bytes accessed | tf_op | source)
XLA Modules:
  0.0 63.1 jit_solution(8615900086507865022)
XLA Ops:
  0.0 57.0 %shard_map.172.strips_hbm = bf16[8,2,2,16,16,128]{5,4,3,2,1,0:T(8,128)(2,1)} custom-call(bf16[2,4096,128]{2,1,0:T(8,128)(2,1)} %strip_hbm.1, bf16[64,128,128]{2,1,0:T(8,128)(2,1)} %constant.17.clone.second_hbm, s32[8]{0:T(128)} %offs_hbm.1, f32[2,8]{1,0:T(2,128)} %constant.23.clone.rest_1_.turn_hbm, f32[32,128]{1,0:T(8,128)} %bitcast.13, f32[1,128]{1,0:T(1,128)} %bitcast.15, ...), custom_call_target="tpu_custom_call" | custom-call | tf_op jit(solution)/shard_map/pallas_call | solution.py:872
  57.0 6.1 %shard_map.173 = bf16[2,4096,128]{2,1,0:T(8,128)(2,1)} custom-call(s32[8]{0:T(128)} %offs_hbm.1, f32[2,8]{1,0:T(2,128)} %constant.23.clone.rest_1_.turn_hbm, f32[32,128]{1,0:T(8,128)} %bitcast.14, f32[1,128]{1,0:T(1,128)} %bitcast.16, bf16[128,128]{1,0:T(8,128)(2,1)} %constant.16.clone.rest_4_.first_hbm, ...), custom_call_target="tpu_custom_call" | custom-call | tf_op jit(solution)/shard_map/pallas_call | solution.py:878
